TPU v7x, 128 devices: a whole 4x4x4 slice. The times are simulated.
128 devices in a mesh: visit: 8 (over x, core), patch: 16 (over y, z).
Axes of the slice: x: 4, y: 4, z: 4, core: 2. Of those that a mesh axis runs over, the one named last changes fastest.
Arguments:
- images: bfloat16 [1024, 512, 512], P(('visit', 'patch')), may hold values from -10 to 10
- warp_rows: bfloat16 [1024, 512, 512], P(('visit', 'patch')), may hold values from -2 to 2
- warp_cols: bfloat16 [1024, 512, 512], P(('visit', 'patch')), may hold values from -2 to 2
- tile_weight: bfloat16 [1024], P(('visit', 'patch')), may hold values from 0.5 to 4
- tile_patch: int32 [1024], P(('visit', 'patch')), may hold values from 0 to 15, as said below
- match_rows: float32 [16, 512, 512], P('patch'), may hold values from -2 to 2
- match_cols: float32 [16, 512, 512], P('patch'), may hold values from -2 to 2
- src_row: int32 [16, 512], P('patch'), may hold values from 0 to 511
- src_col: int32 [16, 512], P('patch'), may hold values from 0 to 511
Outputs:
- coadd: float32 [16, 512, 512], P('patch', 'visit')
- zero_point: float32 [32], P('visit')
- flux_resid: float32 [1024, 512], P(('visit', 'patch'))
Inputs may be any that keep to these rules, and one draw needn't show every extreme that they name: `tile_patch`: among the 8 tiles of one device no patch is named more than 2 times; in each visit row one patch is named exactly 2 times by every device of the row; every patch is named by some tile of every visit row.
All inputs are finite; a program needn't handle non-finite values.
Results may differ from a plain program's by a relative error of at most 0.0065.
Values may be sent and summed in bfloat16 or wider, within the bound.
A program may use at most 128 MiB of HBM per device.

v0:
```python
import jax
import jax.numpy as jnp
from jax import lax
from jax.sharding import PartitionSpec as P

VIS_ROW = 4
CAP = 2


HIGHEST = lax.Precision.HIGHEST
APERTURE = 2.5


def profiles(centers, length):
    pixel_grid = jnp.arange(length).astype(jnp.float32)
    distance = pixel_grid[None, :] - centers.astype(jnp.float32)[:, None]
    return jnp.exp(-distance * distance / (2.0 * APERTURE * APERTURE)).astype(jnp.bfloat16)


def measure(received, row_block, col_prof):
    by_column = jnp.einsum("nyx,qx->nyq", received, col_prof, preferred_element_type=jnp.float32)
    return jnp.einsum("nyq,qy->nq", by_column, row_block.astype(jnp.float32), precision=HIGHEST)


def coadd_flux(matched, row_block, col_prof):
    by_column = jnp.dot(matched, col_prof.astype(jnp.float32).T, precision=HIGHEST)
    return jnp.einsum("yq,qy->q", by_column, row_block.astype(jnp.float32), precision=HIGHEST)


def match_after(stacked_share, kernel_rows, kernel_cols, row_offset, row_share):
    partial_value = jnp.dot(stacked_share, kernel_cols.T, precision=HIGHEST)
    own_rows = lax.dynamic_slice_in_dim(kernel_rows, row_offset, row_share, 0)
    return jnp.dot(
        own_rows, lax.all_gather(partial_value, "visit", axis=0, tiled=True), precision=HIGHEST
    )


def shards(
    images, warp_rows, warp_cols, tile_weight, tile_patch, match_rows, match_cols, src_row, src_col
):
    tile_count, tile_side, _ = images.shape
    visit_count = lax.axis_size("visit")
    patch_count = lax.axis_size("patch")
    row_share = tile_side // visit_count
    row_offset = lax.axis_index("visit") * row_share
    half_warp = jnp.einsum(
        "tij,tkj->tik", images, warp_cols, preferred_element_type=jnp.float32
    ).astype(jnp.bfloat16)
    warped = jnp.einsum(
        "tij,tjk->tik", warp_rows, half_warp, preferred_element_type=jnp.float32
    ).astype(jnp.bfloat16)
    tile_order = jnp.arange(tile_count)
    same_patch = (tile_patch[:, None] == tile_patch[None, :]) & (
        tile_order[None, :] < tile_order[:, None]
    )
    slot_index = jnp.sum(same_patch.astype(jnp.int32), axis=1)
    target = tile_patch * CAP + slot_index
    row_prof = profiles(src_row[0], tile_side)
    col_prof = profiles(src_col[0], tile_side)
    source_count = row_prof.shape[0]
    kernel_rows = match_rows[0]
    kernel_cols = match_cols[0]
    outgoing_weight = jnp.zeros((patch_count * CAP,), jnp.bfloat16).at[target].set(tile_weight)
    row_block = lax.dynamic_slice_in_dim(row_prof, row_offset, row_share, 1)
    outgoing = (
        jnp.zeros((patch_count * CAP, tile_side, tile_side), jnp.bfloat16).at[target].set(warped)
    )
    received, received_weight = (
        lax.all_to_all(
            outgoing.reshape(patch_count, CAP, tile_side, tile_side),
            "patch",
            split_axis=0,
            concat_axis=0,
            tiled=True,
        ),
        lax.all_to_all(
            outgoing_weight.reshape(patch_count, CAP),
            "patch",
            split_axis=0,
            concat_axis=0,
            tiled=True,
        ),
    )
    received = received.reshape(patch_count * CAP, tile_side, tile_side)
    received_weight = received_weight.reshape(-1).astype(jnp.float32)
    stacked = jnp.sum(received_weight[:, None, None] * received.astype(jnp.float32), axis=0)
    weight_part = jnp.sum(received_weight)
    fluxes = measure(received, row_prof, col_prof)
    stacked_share = lax.psum_scatter(stacked, "visit", scatter_dimension=0, tiled=True)
    matched = match_after(stacked_share, kernel_rows, kernel_cols, row_offset, row_share)
    flux_part = coadd_flux(matched, row_block, col_prof)
    weight_all, flux_all = lax.psum((weight_part, flux_part), "visit")
    coadd = matched / weight_all
    ref_flux = flux_all / weight_all
    returned, returned_template = (
        lax.all_to_all(
            fluxes.reshape(patch_count, CAP, source_count),
            "patch",
            split_axis=0,
            concat_axis=0,
            tiled=True,
        ),
        lax.all_to_all(
            jnp.broadcast_to(ref_flux[None, None, :], (patch_count, 1, source_count)),
            "patch",
            split_axis=0,
            concat_axis=0,
            tiled=True,
        ),
    )
    tile_flux = returned.reshape(patch_count * CAP, source_count)[target]
    tile_ref = returned_template.reshape(patch_count, source_count)[tile_patch]
    visit_local = tile_order % VIS_ROW
    visit_pick = (visit_local[:, None] == jnp.arange(VIS_ROW)[None, :]).astype(jnp.float32)
    numerator = jnp.dot(visit_pick.T, jnp.sum(tile_flux * tile_ref, axis=1), precision=HIGHEST)
    denominator = jnp.dot(visit_pick.T, jnp.sum(tile_ref * tile_ref, axis=1), precision=HIGHEST)
    numerator_all, denominator_all = lax.psum((numerator, denominator), "patch")
    zero_point = numerator_all / denominator_all
    flux_resid = tile_flux - zero_point[visit_local][:, None] * tile_ref
    return (coadd[None], zero_point, flux_resid)


def solution(mesh):
    in_specs = (
        P(("visit", "patch"), None, None),
        P(("visit", "patch"), None, None),
        P(("visit", "patch"), None, None),
        P(("visit", "patch")),
        P(("visit", "patch")),
        P("patch", None, None),
        P("patch", None, None),
        P("patch", None),
        P("patch", None),
    )
    out_specs = (P("patch", "visit", None), P("visit"), P(("visit", "patch"), None))
    return jax.shard_map(shards, mesh=mesh, in_specs=in_specs, out_specs=out_specs, check_vma=False)
```

profile of v0, /device:TPU:1, one launch (start us, length us, event | category | flops | bytes accessed | tf_op | source)
XLA Modules:
  0.0 504.7 jit_solution(16662879666464052184)
XLA Ops:
  7.2 0.9 convert_reduce_fusion
  8.8 0.7 scatter_custom_fusion
  10.2 8.6 %all-to-all-start = ((bf16[16,1,2]{2,1,0:T(2,128)(2,1)}), bf16[16,1,2]{2,1,0:T(2,128)(2,1)S(1)}, u32[]{:S(2)}, u32[]{:S(2)}) async-start(bf16[16,1,2]{2,1,0:T(2,128)(2,1)} %all_to_all.20), calls=%async_computation | async-start | bytes 16384 | tf_op jit(solution)/shard_map/all_to_all | solution.py:76
  18.8 11.2 %convert_bitcast_fusion = bf16[8,512,512]{1,2,0:T(8,128)(2,1)} fusion(bf16[8,512,512]{2,1,0:T(8,128)(2,1)} %param.10, bf16[8,512,512]{2,1,0:T(8,128)(2,1)} %param.9, bf16[8,512,512]{2,1,0:T(8,128)(2,1)} %param.11), kind=kOutput, calls=%fused_computation.7 | convolution fusion | flops 4299161600 | bytes 16777216 | tf_op jit(solution)/shard_map/tij,tjk->tik/dot_general | solution.py:49
  30.0 6.5 %copy.27 = bf16[8,512,512]{2,1,0:T(8,128)(2,1)} copy(bf16[8,512,512]{1,2,0:T(8,128)(2,1)} %convert_bitcast_fusion) | data formatting | bytes 8388608 | tf_op jit(solution)/shard_map/convert_element_type | solution.py:51
  36.5 5.9 %broadcast_in_dim.14 = bf16[32,512,512]{2,1,0:T(8,128)(2,1)} broadcast(bf16[]{:T(256)} %constant.37.clone.1), dimensions={} | broadcast | bytes 16777218 | tf_op jit(solution)/shard_map/broadcast_in_dim | solution.py:66
  42.3 10.9 %scatter_fusion = bf16[32,512,512]{2,1,0:T(8,128)(2,1)} fusion(bf16[32,512,512]{2,1,0:T(8,128)(2,1)} %broadcast_in_dim.14, s32[8]{0:T(128)S(1)} %get-tuple-element.12, bf16[8,512,512]{2,1,0:T(8,128)(2,1)} %copy.27), kind=kCustom, calls=%fused_computation.4 | custom fusion | bytes 12582944 | tf_op jit(solution)/shard_map/scatter | solution.py:66
  53.3 6.8 %all-to-all-start.1 = ((bf16[16,2,512,512]{3,2,1,0:T(8,128)(2,1)}), bf16[16,2,512,512]{3,2,1,0:T(8,128)(2,1)}, u32[]{:S(2)}, u32[]{:S(2)}) async-start(bf16[16,2,512,512]{3,2,1,0:T(8,128)(2,1)} %bitcast.45), calls=%async_computation.1 | async-start | bytes 33554432 | tf_op jit(solution)/shard_map/all_to_all | solution.py:69
  60.1 291.5 %all-to-all-done.1 = bf16[16,2,512,512]{3,2,1,0:T(8,128)(2,1)} async-done(((bf16[16,2,512,512]{3,2,1,0:T(8,128)(2,1)}), bf16[16,2,512,512]{3,2,1,0:T(8,128)(2,1)}, u32[]{:S(2)}, u32[]{:S(2)}) %all-to-all-start.1) | async-done | bytes 16777248 | tf_op jit(solution)/shard_map/all_to_all | solution.py:69
  351.6 8.4 %multiply_reduce_fusion.1 = f32[512,512]{1,0:T(8,128)} fusion(bf16[16,2,512,512]{3,2,1,0:T(8,128)(2,1)} %all-to-all-done.1, f32[16,2]{1,0:T(8,128)S(1)} %bitcast.48), kind=kLoop, calls=%fused_computation.6 | loop fusion | flops 24903680 | bytes 17825920 | tf_op jit(solution)/shard_map/reduce_sum | solution.py:86
  360.4 1.1 fusion.20
  362.5 35.3 %reduce-scatter.2.cloned.1.call-done = f32[64,512]{1,0:T(8,128)} async-done(((f32[512,512]{1,0:T(8,128)}), f32[64,512]{1,0:T(8,128)}) %reduce-scatter.2.cloned.1.call-update) | async-done | bytes 131088 | tf_op jit(solution)/shard_map/reduce_scatter | solution.py:89
  397.7 2.7 fusion.12
  400.4 15.2 %multiply_reduce_fusion = f32[512,32]{0,1:T(8,128)S(1)} fusion(f32[512,512]{0,1:T(8,128)S(1)} %copy.42, bf16[32,512,512]{2,1,0:T(8,128)(2,1)} %bitcast.9, f32[512]{0:T(512)S(1)} %bitcast.50, f32[512]{0:T(512)S(1)} %iota_convert_fusion), kind=kOutput, calls=%fused_computation.5 | convolution fusion | flops 8608006144 | bytes 17895424 | tf_op jit(solution)/shard_map/nyx,qx->nyq/dot_general | solution.py:21
  416.3 9.4 %all-gather.2.cloned.1.call-done = f32[512,512]{1,0:T(8,128)} async-done(((f32[64,512]{1,0:T(8,128)}), f32[512,512]{1,0:T(8,128)}) %all-gather.2.cloned.1.call-update) | async-done | bytes 1048592 | tf_op jit(solution)/shard_map/all_gather | solution.py:34
  425.7 2.1 fusion.17
  427.8 0.8 convolution_bitcast_fusion
  428.7 1.1 multiply_reduce_fusion.2
  429.8 6.7 %all-to-all-start.2 = ((f32[16,2,512]{2,1,0:T(2,128)}), f32[16,2,512]{2,1,0:T(2,128)S(1)}, u32[]{:S(2)}, u32[]{:S(2)}) async-start(f32[16,2,512]{2,1,0:T(2,128)} %reshape.93), calls=%async_computation.3 | async-start | bytes 131072 | tf_op jit(solution)/shard_map/all_to_all | solution.py:96
  436.6 13.0 %all-reduce.1 = (f32[]{:T(128)}, f32[512]{0:T(512)S(1)}) all-reduce(f32[]{:T(128)} %convert_reduce_fusion.1, f32[512]{0:T(512)S(1)} %multiply_reduce_fusion.2), channel_id=1, replica_groups=mesh['visit'=8,'patch'=16] {'visit'}, use_global_device_ids=true, to_apply=%region_6.0 | all-reduce | flops 513 | bytes 4104 | tf_op jit(solution)/shard_map/psum | solution.py:92
  450.8 6.9 %all-to-all-start.3 = ((f32[16,1,512]{2,1,0:T(1,128)}), f32[16,1,512]{2,1,0:T(1,128)S(1)}, u32[]{:S(2)}, u32[]{:S(2)}) async-start(f32[16,1,512]{2,1,0:T(1,128)} %broadcast_in_dim.16), calls=%async_computation.4 | async-start | bytes 65536 | tf_op jit(solution)/shard_map/all_to_all | solution.py:103
  458.4 5.8 %all-to-all-done.3 = f32[16,1,512]{2,1,0:T(1,128)S(1)} async-done(((f32[16,1,512]{2,1,0:T(1,128)}), f32[16,1,512]{2,1,0:T(1,128)S(1)}, u32[]{:S(2)}, u32[]{:S(2)}) %all-to-all-start.3) | async-done | bytes 32800 | tf_op jit(solution)/shard_map/all_to_all | solution.py:103
  465.2 1.3 divide_bitcast_fusion
  466.5 30.0 %all-reduce = (f32[4]{0:T(128)S(1)}, f32[4]{0:T(128)S(1)}) all-reduce(f32[4]{0:T(128)S(1)} %convolution_bitcast_fusion.2, f32[4]{0:T(128)S(1)} %convolution_bitcast_fusion.1), channel_id=1, replica_groups=mesh['visit'=8,'patch'=16] {'patch'}, use_global_device_ids=true, to_apply=%region_9.10 | all-reduce | flops 8 | bytes 64 | tf_op jit(solution)/shard_map/psum | solution.py:117
  (40 shorter events, 7.6 us)
Async XLA Ops:
  7.2 390.6 %copy-start = (f32[1,512,512]{2,1,0:T(8,128)S(1)}, f32[1,512,512]{2,1,0:T(8,128)}, u32[]{:S(2)}) copy-start(f32[1,512,512]{2,1,0:T(8,128)} %param.15) | copy-start | bytes 3145732
  10.2 43.0 %all-to-all-start = ((bf16[16,1,2]{2,1,0:T(2,128)(2,1)}), bf16[16,1,2]{2,1,0:T(2,128)(2,1)S(1)}, u32[]{:S(2)}, u32[]{:S(2)}) async-start(bf16[16,1,2]{2,1,0:T(2,128)(2,1)} %all_to_all.20), calls=%async_computation | async-start | bytes 16384 | tf_op jit(solution)/shard_map/all_to_all | solution.py:76
  53.3 298.3 %all-to-all-start.1 = ((bf16[16,2,512,512]{3,2,1,0:T(8,128)(2,1)}), bf16[16,2,512,512]{3,2,1,0:T(8,128)(2,1)}, u32[]{:S(2)}, u32[]{:S(2)}) async-start(bf16[16,2,512,512]{3,2,1,0:T(8,128)(2,1)} %bitcast.45), calls=%async_computation.1 | async-start | bytes 33554432 | tf_op jit(solution)/shard_map/all_to_all | solution.py:69
  60.0 337.7 %reduce-scatter.2.cloned.1.call-start = ((), (), s32[]{:S(2)}) async-start(), calls=%async_computation.5 | async-start | bytes 1179648 | tf_op jit(solution)/shard_map/reduce_scatter | solution.py:89
  351.6 8.7 %copy-start.2 = (s32[1,512]{1,0:T(1,128)S(1)}, s32[1,512]{1,0:T(1,128)}, u32[]{:S(2)}) copy-start(s32[1,512]{1,0:T(1,128)} %param.17) | copy-start | bytes 6148
  351.6 8.7 %copy-start.3 = (s32[1,512]{1,0:T(1,128)S(1)}, s32[1,512]{1,0:T(1,128)}, u32[]{:S(2)}) copy-start(s32[1,512]{1,0:T(1,128)} %param.16) | copy-start | bytes 6148
  360.1 65.7 %all-gather.2.cloned.1.call-start = ((), (), s32[]{:S(2)}) async-start(), calls=%async_computation.6 | async-start | bytes 1179648 | tf_op jit(solution)/shard_map/all_gather | solution.py:34
  429.8 20.4 %all-to-all-start.2 = ((f32[16,2,512]{2,1,0:T(2,128)}), f32[16,2,512]{2,1,0:T(2,128)S(1)}, u32[]{:S(2)}, u32[]{:S(2)}) async-start(f32[16,2,512]{2,1,0:T(2,128)} %reshape.93), calls=%async_computation.3 | async-start | bytes 131072 | tf_op jit(solution)/shard_map/all_to_all | solution.py:96
  450.8 13.4 %all-to-all-start.3 = ((f32[16,1,512]{2,1,0:T(1,128)}), f32[16,1,512]{2,1,0:T(1,128)S(1)}, u32[]{:S(2)}, u32[]{:S(2)}) async-start(f32[16,1,512]{2,1,0:T(1,128)} %broadcast_in_dim.16), calls=%async_computation.4 | async-start | bytes 65536 | tf_op jit(solution)/shard_map/all_to_all | solution.py:103
  496.5 1.3 copy-start.1
Sparse Core Ops, SparseCore 0:
  360.2 37.4 reduce-scatter.1
  400.6 25.1 all-gather.1
where the time goes:
time: 515 us; the launch traced here: 505 us
  waiting for transfers between devices  342 us (66%)
  blocking collectives  42.9 us (8%)
  matrix products  32.1 us (6%)
  starting transfers between devices  29.3 us (6%)
  local copies, waits for them, and re-layouts  28.3 us (5%)
  other arithmetic  15.8 us (3%)
  between operations  14.2 us (3%)
    all_to_all x1, waiting for transfers between devices, shards(): lax.all_to_all(outgoing.reshape(patch_count, CAP, tile_side, tile_side),...  291 us
    reduce_scatter x1, waiting for transfers between devices, shards(): lax.psum_scatter(stacked, 'visit', scatter_dimension=0, tiled=True)  35.3 us
    psum x1, blocking collectives, shards(): numerator_all, denominator_all = lax.psum((numerator, denominator), 'patch')  30 us
    dot_general x1, matrix products, measure(): jnp.einsum('nyx,qx->nyq', received, col_prof, preferred_element_type=jnp....  15.2 us
    psum x1, blocking collectives, shards(): weight_all, flux_all = lax.psum((weight_part, flux_part), 'visit')  13 us
    dot_general x1, matrix products, shards(): jnp.einsum('tij,tjk->tik', warp_rows, half_warp, preferred_element_type=j...  11.2 us
    scatter x1, local copies, waits for them, and re-layouts, shards(): jnp.zeros((patch_count * CAP, tile_side, tile_side), jnp.bfloat16)  10.9 us
  transfers between devices with their start and end apart: 6, of which 4 were waited for; matrix products, arithmetic and copies ran while one was open for 11% of the time, Pallas kernels for 0%

commit v1 on v0

v1 whole, which is shorter than its diff:
```python
import jax
import jax.numpy as jnp
from jax import lax
from jax.experimental import pallas as pl
from jax.experimental.pallas import tpu as pltpu
from jax.sharding import PartitionSpec as P

F32 = jnp.float32
BF16 = jnp.bfloat16
S = 512
NP = 16
NV = 8
TD = 8
MESH = pl.DeviceIdType.MESH

ORDER = ("x0", "y0", "z0", "x1", "y1", "z1")
ROWS = (48, 48, 48, 48, 32, 32)
OFFS = (0, 48, 96, 144, 192, 224)
PIECES = (
    ((0, 0, 48, 0),),
    ((0, 48, 16, 0), (1, 0, 32, 16)),
    ((1, 32, 32, 0), (2, 0, 16, 32)),
    ((2, 16, 48, 0),),
    ((3, 0, 32, 0),),
    ((3, 32, 32, 0),),
)


def gray(c):
    return c // 2, (c // 2 + c % 2) % 2


def nt(a, b):
    return lax.dot_general(a, b, (((1,), (1,)), ((), ())), preferred_element_type=F32)


def tn(a, b):
    return lax.dot_general(a, b, (((0,), (0,)), ((), ())), preferred_element_type=F32)


def nn(a, b):
    return jnp.dot(a, b, preferred_element_type=F32)


def split(a):
    high = a.astype(BF16)
    return high, (a - high.astype(F32)).astype(BF16)


def profile(center, first, count):
    pixel = lax.broadcasted_iota(jnp.int32, (count, S), 0).astype(F32) + first
    distance = pixel - center
    return jnp.exp(distance * distance * (-1.0 / 12.5)).astype(BF16)


def kernel(
    patch_sm, weight_sm, warped_hbm, mr_hbm, mc_hbm, srow_ref, scol_ref,
    coadd_ref, zp_ref, resid_ref,
    warped, mr, mc, acc, rc, r0, r1, r2, fin, r3, r4, r5,
    metag, fluxg, pg, refg, sg, colt, rowt, bth, btl, at, mch, mcl, mrow, sblk,
    tab_i, tab_w, lsem, csem_s, csem_r, rsem_s, rsem_r, gsem_s, gsem_r, vsem_s, vsem_r, asem_s, asem_r,
):
    v = lax.axis_index("visit")
    me = lax.axis_index("patch")
    x, core = v // 2, v % 2
    y, z = me // 4, me % 4
    side = {}
    for name, c in (("x", x), ("y", y), ("z", z)):
        side[name + "1"], side[name + "0"] = gray(c)
    flip0 = lambda c: c + 1 - 2 * (c % 2)
    partner = {
        "x0": (flip0(x) * 2 + core, me), "x1": ((3 - x) * 2 + core, me),
        "y0": (v, flip0(y) * 4 + z), "y1": (v, (3 - y) * 4 + z),
        "z0": (v, y * 4 + flip0(z)), "z1": (v, y * 4 + 3 - z),
    }
    other = 1 - core
    mate = (x * 2 + other, me)

    def remote(src, dst, ss, rs, where):
        return pltpu.make_async_remote_copy(
            src_ref=src, dst_ref=dst, send_sem=ss, recv_sem=rs,
            device_id={"visit": where[0], "patch": where[1]}, device_id_type=MESH,
        )

    barrier = pltpu.get_barrier_semaphore()

    @pl.loop(1, NP)
    def _(o):
        pl.semaphore_signal(barrier, inc=1, device_id={"visit": v, "patch": (me + o) % NP}, device_id_type=MESH)

    @pl.loop(1, NV)
    def _(o):
        pl.semaphore_signal(barrier, inc=1, device_id={"visit": (v + o) % NV, "patch": me}, device_id_type=MESH)

    load_w = pltpu.make_async_copy(warped_hbm, warped, lsem.at[0])
    load_w.start()
    load_r = pltpu.make_async_copy(mr_hbm, mr, lsem.at[1])
    load_r.start()
    load_c = pltpu.make_async_copy(mc_hbm, mc, lsem.at[2])
    load_c.start()

    @pl.loop(0, NP)
    def _(p):
        ia = jnp.int32(0)
        ib = jnp.int32(0)
        wa = jnp.float32(0)
        wb = jnp.float32(0)
        seen = jnp.int32(0)
        for t in range(TD):
            hit = (patch_sm[t] == p).astype(jnp.int32)
            first = hit * (1 - jnp.minimum(seen, 1))
            second = hit * (seen == 1).astype(jnp.int32)
            ia = ia + first * t
            ib = ib + second * t
            wa = wa + first.astype(F32) * weight_sm[t]
            wb = wb + second.astype(F32) * weight_sm[t]
            seen = seen + hit
        tab_i[p] = ia
        tab_i[NP + p] = ib
        tab_w[p] = wa
        tab_w[NP + p] = wb

    for t in range(TD):
        metag[me, t : t + 1, :] = jnp.full((1, 128), patch_sm[t].astype(F32), F32)
        metag[me, TD + t : TD + t + 1, :] = jnp.full((1, 128), weight_sm[t], F32)
    for c in range(4):
        metag[me, 16 + c : 17 + c, :] = srow_ref[:, c * 128 : (c + 1) * 128].astype(F32)
        metag[me, 20 + c : 21 + c, :] = scol_ref[:, c * 128 : (c + 1) * 128].astype(F32)

    pl.semaphore_wait(barrier, NP - 1 + NV - 1)

    def gather_copy(buf, kind, o):
        return remote(buf.at[me], buf.at[me], gsem_s.at[kind, o], gsem_r.at[kind, o], (v, (me + o) % NP))

    def gather_start(buf, kind):
        @pl.loop(1, NP)
        def _(o):
            gather_copy(buf, kind, o).start()

    def gather_wait(buf, kind):
        @pl.loop(1, NP)
        def _(o):
            theirs = (me - o + NP) % NP
            remote(buf.at[theirs], buf.at[theirs], gsem_s.at[kind, o], gsem_r.at[kind, o], (v, (me + o) % NP)).wait()

    gather_start(metag, 0)

    def combine(h):
        @pl.loop(0, NP)
        def _(p):
            ia, ib = tab_i[p], tab_i[NP + p]
            wa = jnp.full((16, 128), tab_w[p], F32).astype(BF16)
            wb = jnp.full((16, 128), tab_w[NP + p], F32).astype(BF16)
            bits = {}
            bits["y1"], bits["y0"] = gray(p // 4)
            bits["z1"], bits["z0"] = gray(p % 4)
            for xr in range(4):
                bits["x1"], bits["x0"] = gray(xr)
                for k in range(6):
                    place = 0
                    for j in range(6):
                        place = place * 2 + bits[ORDER[(k + j) % 6]]
                    for tile, first, count, to in PIECES[k]:
                        for i in range(0, count, 16):
                            rows = pl.ds(pl.multiple_of((xr * 2 + h) * 64 + first + i, 16), 16)
                            lanes = slice(tile * 128, tile * 128 + 128)
                            acc[h, place, OFFS[k] + to + i : OFFS[k] + to + i + 16, :] = (
                                warped[ia, rows, lanes] * wa + warped[ib, rows, lanes] * wb
                            )

    load_w.wait()
    combine(other)

    def core_copy(k):
        rows = pl.ds(OFFS[k], ROWS[k])
        return remote(acc.at[other, :, rows, :], rc.at[:, rows, :], csem_s.at[k], csem_r.at[k], mate)

    for k in range(6):
        core_copy(k).start()
    combine(core)
    gather_wait(metag, 0)

    def source_lines(q, first):
        return jnp.concatenate([metag[q, first + c : first + c + 1, :] for c in range(4)], axis=1)

    def measure(first, last):
        @pl.loop(first, last)
        def _(t):
            q = patch_sm[t]
            row_of = source_lines(q, 16)
            col_of = source_lines(q, 20)

            @pl.loop(0, 4)
            def _(b):
                start = pl.multiple_of(b * 128, 128)
                colt[pl.ds(start, 128), :] = profile(col_of, (b * 128).astype(F32), 128)

            def part(b, total):
                start = pl.multiple_of(b * 128, 128)
                by_col = nn(warped[t, pl.ds(start, 128), :], colt[...])
                rows = profile(row_of, (b * 128).astype(F32), 128).astype(F32)
                return total + jnp.sum((by_col * rows).reshape(16, 8, S), axis=0)

            total = lax.fori_loop(0, 4, part, jnp.zeros((8, S), F32))
            fluxg[me, pl.ds(t, 1), :] = jnp.sum(total, axis=0, keepdims=True)

    bufs = (r0, r1, r2, r3, r4, r5)

    def base_of(k, j):
        lo = 0 if j < 3 else 3
        base = 0
        for i in range(lo, j):
            base = base + side[ORDER[(k + i) % 6]] * (32 >> i)
        return base

    def round_copy(k, j):
        d = ORDER[(k + j) % 6]
        half = 32 >> j
        start = base_of(k, j) + (1 - side[d]) * half
        rows = pl.ds(OFFS[k], ROWS[k])
        src = acc.at[core, pl.ds(start, half), rows, :] if j < 3 else fin.at[pl.ds(start, half), rows, :]
        return remote(src, bufs[j].at[:, rows, :], rsem_s.at[j, k], rsem_r.at[j, k], partner[d])

    def round_add(k, j):
        half = 32 >> j
        keep = base_of(k, j + 1) if j != 2 else base_of(k, 2) + side[ORDER[(k + 2) % 6]] * half
        rows = pl.ds(OFFS[k], ROWS[k])
        step = min(half, 8)

        @pl.loop(0, half // step)
        def _(i):
            new = bufs[j][pl.ds(i * step, step), rows, :]
            at_ = pl.ds(keep + i * step, step)
            if j < 2:
                acc[core, at_, rows, :] = acc[core, at_, rows, :] + new
            elif j == 2:
                fin[pl.ds(i * step, step), rows, :] = acc[core, at_, rows, :].astype(F32) + new.astype(F32)
            else:
                fin[at_, rows, :] = fin[at_, rows, :] + new

    def core_add(k):
        rows = pl.ds(OFFS[k], ROWS[k])

        @pl.loop(0, 8)
        def _(i):
            at_ = pl.ds(i * 8, 8)
            acc[core, at_, rows, :] = acc[core, at_, rows, :] + rc[at_, rows, :]

    measure(0, 2)
    for k in range(6):
        core_copy(k).wait()
        core_add(k)
        round_copy(k, 0).start()
    measure(2, 6)
    for k in range(6):
        round_copy(k, 0).wait()
        round_add(k, 0)
        round_copy(k, 1).start()
    measure(6, 8)
    gather_start(fluxg, 1)
    for k in range(6):
        round_copy(k, 1).wait()
        round_add(k, 1)
        round_copy(k, 2).start()

    own_row = source_lines(me, 16)
    own_col = source_lines(me, 20)

    @pl.loop(0, 4)
    def _(b):
        start = pl.multiple_of(b * 128, 128)
        colt[pl.ds(start, 128), :] = profile(own_col, (b * 128).astype(F32), 128)
        rowt[pl.ds(start, 128), :] = profile(own_row, (b * 128).astype(F32), 128)

    load_r.wait()
    load_c.wait()

    @pl.loop(0, 4)
    def _(b):
        start = pl.multiple_of(b * 128, 128)
        cols = pl.ds(start, 128)
        high, low = split(mc[:, cols])
        value = tn(high, colt[...]) + tn(low, colt[...])
        high, low = split(value)
        bth[cols, :] = high
        btl[cols, :] = low
        high, low = split(mr[:, cols])
        at[cols, :] = tn(high, rowt[...]) + tn(low, rowt[...])
        high, low = split(mc[cols, :])
        mch[cols, :] = high
        mcl[cols, :] = low

    for j in range(2, 5):
        for k in range(6):
            round_copy(k, j).wait()
            round_add(k, j)
            round_copy(k, j + 1).start()
    for k in range(6):
        round_copy(k, 5).wait()
        place = base_of(k, 6)
        for tile, first, count, to in PIECES[k]:
            here = slice(OFFS[k] + to, OFFS[k] + to + count)
            sblk[first : first + count, tile * 128 : tile * 128 + 128] = fin[place, here, :] + r5[0, here, :]

    own = pl.ds(pl.multiple_of(v * 64, 64), 64)
    sg[own, :] = sblk[...].astype(BF16)

    def rows_of(who):
        return pl.ds(pl.multiple_of(who * 64, 64), 64)

    def share_copy(o):
        if o == 0:
            return remote(sg.at[own, :], sg.at[own, :], asem_s.at[0], asem_r.at[0], mate)
        return remote(sg.at[own, :], sg.at[own, :], asem_s.at[o], asem_r.at[o], (((x + o) % 4) * 2 + core, me))

    def pass_copy(o):
        rows = rows_of(((x - o + 4) % 4) * 2 + core)
        return remote(sg.at[rows, :], sg.at[rows, :], asem_s.at[3 + o], asem_r.at[3 + o], mate)

    high, low = split(sblk[...])
    value = nn(high, bth[...]) + nn(low, bth[...]) + nn(high, btl[...])
    partial = jnp.sum(value * at[own, :], axis=0, keepdims=True)
    for c in range(4):
        pg[v, c : c + 1, :] = partial[:, c * 128 : (c + 1) * 128]
    mine = metag[:, 0:8, :].reshape(128, 128) == me.astype(F32)
    weights = jnp.where(mine, metag[:, 8:16, :].reshape(128, 128), 0.0)
    pg[v, 4:5, :] = jnp.sum(weights, axis=0, keepdims=True)
    pg[v, 5:8, :] = jnp.zeros((3, 128), F32)

    @pl.loop(1, NV)
    def _(o):
        remote(pg.at[v], pg.at[v], vsem_s.at[o], vsem_r.at[o], ((v + o) % NV, me)).start()

    for o in (1, 3, 2, 0):
        share_copy(o).start()

    gather_wait(fluxg, 1)
    tile = lax.broadcasted_iota(jnp.int32, (128, 128), 0)
    lane = lax.broadcasted_iota(jnp.int32, (128, 128), 1)
    hits = (metag[:, 0:8, :].reshape(128, 128) == (lane % 16).astype(F32)) & (tile % 4 == lane // 16)
    hits = jnp.where(hits, 1.0, 0.0).astype(BF16)
    high, low = split(fluxg[...].reshape(128, S))
    sums = tn(hits, high) + tn(hits, low)
    counts = tn(hits, jnp.ones((128, 128), BF16))

    @pl.loop(1, NV)
    def _(o):
        theirs = (v - o + NV) % NV
        remote(pg.at[theirs], pg.at[theirs], vsem_s.at[o], vsem_r.at[o], ((v + o) % NV, me)).wait()

    total = jnp.sum(pg[...], axis=0)
    inverse = 1.0 / total[4:5, :]
    refg[me] = total * inverse
    gather_start(refg, 2)

    for o in (1, 3, 2):
        rows = rows_of(((x - o + 4) % 4) * 2 + core)
        remote(sg.at[rows, :], sg.at[rows, :], asem_s.at[o], asem_r.at[o], (((x + o) % 4) * 2 + core, me)).wait()
        pass_copy(o).start()
    mates = rows_of(x * 2 + other)
    remote(sg.at[mates, :], sg.at[mates, :], asem_s.at[0], asem_r.at[0], mate).wait()
    for o in (1, 3, 2):
        rows = rows_of(((x - o + 4) % 4) * 2 + other)
        remote(sg.at[rows, :], sg.at[rows, :], asem_s.at[3 + o], asem_r.at[3 + o], mate).wait()
    high, low = split(mr[own, :])
    matched = nn(high, sg[...]) + nn(low, sg[...])
    high, low = split(matched)
    matched = nt(high, mch[...]) + nt(low, mch[...]) + nt(high, mcl[...])
    for c in range(4):
        coadd_ref[:, c * 128 : (c + 1) * 128] = matched[:, c * 128 : (c + 1) * 128] * inverse

    gather_wait(refg, 2)
    refs = jnp.concatenate([refg[:, c, :] for c in range(4)], axis=1)
    squares = jnp.sum(refs * refs, axis=1, keepdims=True)
    fits = []
    for u in range(4):
        rows = slice(u * 16, u * 16 + 16)
        top = jnp.sum(jnp.sum(sums[rows, :] * refs, axis=0, keepdims=True), axis=1, keepdims=True)
        low = jnp.sum(counts[rows, 0:1] * squares, axis=0, keepdims=True)
        fits.append(top / low)
    for u in range(4):
        zp_ref[u : u + 1, :] = jnp.broadcast_to(fits[u], (1, 128))
    for t in range(TD):
        q = patch_sm[t]
        template = jnp.concatenate([refg[q, c : c + 1, :] for c in range(4)], axis=1)
        resid_ref[t : t + 1, :] = fluxg[me, t : t + 1, :] - fits[t % 4] * template


def fused(tile_patch, tile_weight, warped, match_rows, match_cols, src_row, src_col):
    dma = pltpu.SemaphoreType.DMA
    any_ = pl.BlockSpec(memory_space=pl.ANY)
    smem = pl.BlockSpec(memory_space=pltpu.SMEM)
    vmem = pl.BlockSpec(memory_space=pltpu.VMEM)
    return pl.pallas_call(
        kernel,
        out_shape=(
            jax.ShapeDtypeStruct((64, S), F32),
            jax.ShapeDtypeStruct((4, 128), F32),
            jax.ShapeDtypeStruct((TD, S), F32),
        ),
        in_specs=[smem, smem, any_, any_, any_, vmem, vmem],
        out_specs=(vmem, vmem, vmem),
        scratch_shapes=[
            pltpu.VMEM((TD, S, S), BF16),
            pltpu.VMEM((S, S), F32),
            pltpu.VMEM((S, S), F32),
            pltpu.VMEM((2, 64, 256, 128), BF16),
            pltpu.VMEM((64, 256, 128), BF16),
            pltpu.VMEM((32, 256, 128), BF16),
            pltpu.VMEM((16, 256, 128), BF16),
            pltpu.VMEM((8, 256, 128), BF16),
            pltpu.VMEM((8, 256, 128), F32),
            pltpu.VMEM((4, 256, 128), F32),
            pltpu.VMEM((2, 256, 128), F32),
            pltpu.VMEM((1, 256, 128), F32),
            pltpu.VMEM((NP, 24, 128), F32),
            pltpu.VMEM((NP, TD, S), F32),
            pltpu.VMEM((NV, 8, 128), F32),
            pltpu.VMEM((NP, 8, 128), F32),
            pltpu.VMEM((S, S), BF16),
            pltpu.VMEM((S, S), BF16),
            pltpu.VMEM((S, S), BF16),
            pltpu.VMEM((S, S), BF16),
            pltpu.VMEM((S, S), BF16),
            pltpu.VMEM((S, S), F32),
            pltpu.VMEM((S, S), BF16),
            pltpu.VMEM((S, S), BF16),
            pltpu.VMEM((64, S), F32),
            pltpu.VMEM((64, S), F32),
            pltpu.SMEM((2 * NP,), jnp.int32),
            pltpu.SMEM((2 * NP,), F32),
            dma((3,)), dma((6,)), dma((6,)), dma((6, 6)), dma((6, 6)),
            dma((3, NP)), dma((3, NP)), dma((NV,)), dma((NV,)), dma((8,)), dma((8,)),
        ],
        compiler_params=pltpu.CompilerParams(
            collective_id=0, has_side_effects=True, vmem_limit_bytes=60 * 1024 * 1024
        ),
        name="coadd",
    )(tile_patch, tile_weight, warped, match_rows, match_cols, src_row, src_col)


def shards(
    images, warp_rows, warp_cols, tile_weight, tile_patch, match_rows, match_cols, src_row, src_col
):
    half_warp = jnp.einsum(
        "tij,tkj->tik", images, warp_cols, preferred_element_type=jnp.float32
    ).astype(jnp.bfloat16)
    warped = jnp.einsum(
        "tij,tjk->tik", warp_rows, half_warp, preferred_element_type=jnp.float32
    ).astype(jnp.bfloat16)
    coadd, zero_point, resid = fused(
        tile_patch, tile_weight.astype(F32), warped, match_rows[0], match_cols[0], src_row, src_col
    )
    return coadd[None], zero_point[:, 0], resid


def solution(mesh):
    in_specs = (
        P(("visit", "patch"), None, None),
        P(("visit", "patch"), None, None),
        P(("visit", "patch"), None, None),
        P(("visit", "patch")),
        P(("visit", "patch")),
        P("patch", None, None),
        P("patch", None, None),
        P("patch", None),
        P("patch", None),
    )
    out_specs = (P("patch", "visit", None), P("visit"), P(("visit", "patch"), None))
    return jax.shard_map(shards, mesh=mesh, in_specs=in_specs, out_specs=out_specs, check_vma=False)
```

time: 515 us -> 80.7 us (0.16); the launches traced: 505 us -> 80.4 us
  waiting for transfers between devices: 342 us -> 0 us
  Pallas kernels: 0 us -> 63.3 us
  blocking collectives: 42.9 us -> 0 us
  starting transfers between devices: 29.3 us -> 0 us
  local copies, waits for them, and re-layouts: 28.3 us -> 4.17 us
  matrix products: 32.1 us -> 11.1 us
  other arithmetic: 15.8 us -> 1.17 us
  between operations: 14.2 us -> 0.64 us
    all_to_all x4 -> x0, waiting for transfers between devices: 297 us -> none  [the longest x1 291 us: shards(): lax.all_to_all(outgoing.reshape(patch_count, CAP, tile_side, tile_side),...]
    pallas_call x0 -> x1, Pallas kernels: none -> 63.3 us  [fused(): pl.pallas_call(kernel, out_shape=(jax.ShapeDtypeStruct((64, S), F32), jax...]
    psum x2 -> x0, blocking collectives: 42.9 us -> none  [the longest x1 30 us: shards(): numerator_all, denominator_all = lax.psum((numerator, denominator), 'patch')]
    reduce_scatter x1 -> x0, waiting for transfers between devices: 35.3 us -> none  [shards(): lax.psum_scatter(stacked, 'visit', scatter_dimension=0, tiled=True)]
    all_to_all x4 -> x0, starting transfers between devices: 29 us -> none  [the longest x1 8.59 us: shards(): lax.all_to_all(outgoing_weight.reshape(patch_count, CAP), 'patch', split_...]
    dot_general x6 -> x0, matrix products: 21 us -> none  [the longest x1 15.2 us: measure(): jnp.einsum('nyx,qx->nyq', received, col_prof, preferred_element_type=jnp....]
    scatter x2 -> x0, local copies, waits for them, and re-layouts: 11.7 us -> none  [the longest x1 10.9 us: shards(): jnp.zeros((patch_count * CAP, tile_side, tile_side), jnp.bfloat16)]
    reduce_sum x4 -> x0, other arithmetic: 10.2 us -> none  [the longest x1 8.45 us: shards(): jnp.sum(received_weight[:, None, None] * received.astype(jnp.float32), ax...]
  transfers between devices with their start and end apart: 6 -> 0, of which waited for: 4 -> 0; matrix products, arithmetic and copies ran while one was open for 11% -> 0% of each run, Pallas kernels for 0% -> 0%
where the time goes in v1:
time: 80.7 us; the launch traced here: 80.4 us
  Pallas kernels  63.3 us (78%)
  matrix products  11.1 us (14%)
  local copies, waits for them, and re-layouts  4.17 us (5%)
  other arithmetic  1.17 us (1%)
    pallas_call x1, Pallas kernels, fused(): pl.pallas_call(kernel, out_shape=(jax.ShapeDtypeStruct((64, S), F32), jax...  63.3 us
    dot_general x1, matrix products, shards(): jnp.einsum('tij,tjk->tik', warp_rows, half_warp, preferred_element_type=j...  11.1 us
    unnamed x2, local copies, waits for them, and re-layouts  2.89 us

profile of v1, /device:TPU:1, one launch (start us, length us, event | category | flops | bytes accessed | tf_op | source)
XLA Modules:
  0.0 80.4 jit_solution(2480646598450774483)
XLA Ops:
  0.6 1.2 %convert_element_type.11.weight_sm = f32[8]{0:T(128)} convert(bf16[8]{0:T(256)(128)(2,1)} %param.12) | non-fusion elementwise | flops 8 | bytes 48 | tf_op jit(solution)/shard_map/convert_element_type | solution.py:452
  1.8 11.1 %convert_bitcast_fusion.warped_hbm = bf16[8,512,512]{2,1,0:T(8,128)(2,1)} fusion(bf16[8,512,512]{2,1,0:T(8,128)(2,1)} %param.10, bf16[8,512,512]{2,1,0:T(8,128)(2,1)} %param.9, bf16[8,512,512]{2,1,0:T(8,128)(2,1)} %param.11), kind=kOutput, calls=%fused_computation | convolution fusion | flops 4299161600 | bytes 16777216 | tf_op jit(solution)/shard_map/tij,tjk->tik/dot_general | solution.py:448
  12.9 63.3 %coadd.1 = (f32[64,512]{1,0:T(8,128)}, f32[4,128]{1,0:T(4,128)}, f32[8,512]{1,0:T(8,128)}) custom-call(s32[8]{0:T(128)} %patch_sm.1, f32[8]{0:T(128)} %convert_element_type.11.weight_sm, bf16[8,512,512]{2,1,0:T(8,128)(2,1)} %convert_bitcast_fusion.warped_hbm, f32[512,512]{1,0:T(8,128)} %bitcast.8, f32[512,512]{1,0:T(8,128)} %bitcast.9, s32[1,512]{1,0:T(1,128)} %srow_ref.1, ...), custom_call_target="tpu_custom_call" | custom-call | tf_op jit(solution)/shard_map/coadd/pallas_call | solution.py:394
  76.2 1.3 %slice_reduce_fusion = f32[4]{0:T(128)} fusion(f32[4,128]{1,0:T(4,128)} %get-tuple-element.7), kind=kLoop, calls=%fused_computation.4 | loop fusion | bytes 32 | tf_op jit(solution)/shard_map/slice | solution.py:454
  77.5 1.6 %copy.17 = f32[1,64,512]{2,1,0:T(8,128)} copy(f32[1,64,512]{2,1,0:T(8,128)} %bitcast.10) | data formatting | bytes 262144
  79.1 1.3 %copy.18 = f32[8,512]{1,0:T(8,128)} copy(f32[8,512]{1,0:T(8,128)} %get-tuple-element.14) | data formatting | bytes 32768

commit v2 on v1

--- a/solution.py
+++ b/solution.py
@@ -14,15 +14,9 @@
 MESH = pl.DeviceIdType.MESH
 
 ORDER = ("x0", "y0", "z0", "x1", "y1", "z1")
-ROWS = (48, 48, 48, 48, 32, 32)
-OFFS = (0, 48, 96, 144, 192, 224)
-PIECES = (
-    ((0, 0, 48, 0),),
-    ((0, 48, 16, 0), (1, 0, 32, 16)),
-    ((1, 32, 32, 0), (2, 0, 16, 32)),
-    ((2, 16, 48, 0),),
-    ((3, 0, 32, 0),),
-    ((3, 32, 32, 0),),
+ROWS = ((32, 32, 16, 16, 16, 16), (16, 16, 32, 32, 16, 16))
+OFFS = tuple(
+    tuple(s * 128 + sum(ROWS[s][:k]) for k in range(6)) for s in range(2)
 )
 
 
@@ -54,11 +48,11 @@
 
 
 def kernel(
-    patch_sm, weight_sm, warped_hbm, mr_hbm, mc_hbm, srow_ref, scol_ref,
+    patch_sm, weight_ref, img_hbm, wr_hbm, wc_hbm, mr_hbm, mc_hbm, srow_ref, scol_ref,
     coadd_ref, zp_ref, resid_ref,
-    warped, mr, mc, acc, rc, r0, r1, r2, fin, r3, r4, r5,
+    img, wr, wc, halfs, warped, mr, mc, acc, rc, r0, r1, r2, fin, r3, r4, r5,
     metag, fluxg, pg, refg, sg, colt, rowt, bth, btl, at, mch, mcl, mrow, sblk,
-    tab_i, tab_w, lsem, csem_s, csem_r, rsem_s, rsem_r, gsem_s, gsem_r, vsem_s, vsem_r, asem_s, asem_r,
+    tab_i, tab_w, weight_sm, tsem, lsem, csem_s, csem_r, rsem_s, rsem_r, gsem_s, gsem_r, vsem_s, vsem_r, asem_s, asem_r,
 ):
     v = lax.axis_index("visit")
     me = lax.axis_index("patch")
@@ -92,12 +86,23 @@
     def _(o):
         pl.semaphore_signal(barrier, inc=1, device_id={"visit": (v + o) % NV, "patch": me}, device_id_type=MESH)
 
-    load_w = pltpu.make_async_copy(warped_hbm, warped, lsem.at[0])
-    load_w.start()
+    def tile_load(i, t):
+        hbm, buf = ((wc_hbm, wc), (img_hbm, img), (wr_hbm, wr))[i]
+        return pltpu.make_async_copy(hbm.at[t], buf.at[t], tsem.at[i, t])
+
+    @pl.loop(0, TD)
+    def _(t):
+        for i in range(3):
+            tile_load(i, t).start()
+
     load_r = pltpu.make_async_copy(mr_hbm, mr, lsem.at[1])
     load_r.start()
     load_c = pltpu.make_async_copy(mc_hbm, mc, lsem.at[2])
     load_c.start()
+
+    lane8 = lax.broadcasted_iota(jnp.int32, (1, TD), 1)
+    for t in range(TD):
+        weight_sm[t] = jnp.sum(jnp.where(lane8 == t, weight_ref[...].astype(F32), 0.0))
 
     @pl.loop(0, NP)
     def _(p):
@@ -127,8 +132,6 @@
         metag[me, 16 + c : 17 + c, :] = srow_ref[:, c * 128 : (c + 1) * 128].astype(F32)
         metag[me, 20 + c : 21 + c, :] = scol_ref[:, c * 128 : (c + 1) * 128].astype(F32)
 
-    pl.semaphore_wait(barrier, NP - 1 + NV - 1)
-
     def gather_copy(buf, kind, o):
         return remote(buf.at[me], buf.at[me], gsem_s.at[kind, o], gsem_r.at[kind, o], (v, (me + o) % NP))
 
@@ -143,9 +146,22 @@
             theirs = (me - o + NP) % NP
             remote(buf.at[theirs], buf.at[theirs], gsem_s.at[kind, o], gsem_r.at[kind, o], (v, (me + o) % NP)).wait()
 
-    gather_start(metag, 0)
-
-    def combine(h):
+    def warp(first, last, s):
+        cols = slice(s * 256, s * 256 + 256)
+
+        @pl.loop(first // 2, last // 2)
+        def _(tt):
+            for i in range(2):
+                t = tt * 2 + i
+                if s == 0:
+                    for n in range(3):
+                        tile_load(n, t).wait()
+                halfs[i] = nt(img[t], wc[t, cols, :]).astype(BF16)
+            for i in range(2):
+                t = tt * 2 + i
+                warped[t, :, cols] = nn(wr[t], halfs[i]).astype(BF16)
+
+    def combine(h, s):
         @pl.loop(0, NP)
         def _(p):
             ia, ib = tab_i[p], tab_i[NP + p]
@@ -160,25 +176,20 @@
                     place = 0
                     for j in range(6):
                         place = place * 2 + bits[ORDER[(k + j) % 6]]
-                    for tile, first, count, to in PIECES[k]:
-                        for i in range(0, count, 16):
-                            rows = pl.ds(pl.multiple_of((xr * 2 + h) * 64 + first + i, 16), 16)
-                            lanes = slice(tile * 128, tile * 128 + 128)
-                            acc[h, place, OFFS[k] + to + i : OFFS[k] + to + i + 16, :] = (
-                                warped[ia, rows, lanes] * wa + warped[ib, rows, lanes] * wb
-                            )
-
-    load_w.wait()
-    combine(other)
-
-    def core_copy(k):
-        rows = pl.ds(OFFS[k], ROWS[k])
-        return remote(acc.at[other, :, rows, :], rc.at[:, rows, :], csem_s.at[k], csem_r.at[k], mate)
-
-    for k in range(6):
-        core_copy(k).start()
-    combine(core)
-    gather_wait(metag, 0)
+                    for at_ in range(OFFS[s][k], OFFS[s][k] + ROWS[s][k], 16):
+                        rows = pl.ds(pl.multiple_of((xr * 2 + h) * 64 + at_ % 64, 16), 16)
+                        lanes = slice(at_ // 64 * 128, at_ // 64 * 128 + 128)
+                        acc[h, place, at_ : at_ + 16, :] = (
+                            warped[ia, rows, lanes] * wa + warped[ib, rows, lanes] * wb
+                        )
+
+    def core_copy(s, k):
+        rows = pl.ds(OFFS[s][k], ROWS[s][k])
+        return remote(acc.at[other, :, rows, :], rc.at[:, rows, :], csem_s.at[s, k], csem_r.at[s, k], mate)
+
+    def core_start(s):
+        for k in range(6):
+            core_copy(s, k).start()
 
     def source_lines(q, first):
         return jnp.concatenate([metag[q, first + c : first + c + 1, :] for c in range(4)], axis=1)
@@ -213,18 +224,18 @@
             base = base + side[ORDER[(k + i) % 6]] * (32 >> i)
         return base
 
-    def round_copy(k, j):
+    def round_copy(s, k, j):
         d = ORDER[(k + j) % 6]
         half = 32 >> j
         start = base_of(k, j) + (1 - side[d]) * half
-        rows = pl.ds(OFFS[k], ROWS[k])
+        rows = pl.ds(OFFS[s][k], ROWS[s][k])
         src = acc.at[core, pl.ds(start, half), rows, :] if j < 3 else fin.at[pl.ds(start, half), rows, :]
-        return remote(src, bufs[j].at[:, rows, :], rsem_s.at[j, k], rsem_r.at[j, k], partner[d])
-
-    def round_add(k, j):
+        return remote(src, bufs[j].at[:, rows, :], rsem_s.at[j, s * 6 + k], rsem_r.at[j, s * 6 + k], partner[d])
+
+    def round_add(s, k, j):
         half = 32 >> j
         keep = base_of(k, j + 1) if j != 2 else base_of(k, 2) + side[ORDER[(k + 2) % 6]] * half
-        rows = pl.ds(OFFS[k], ROWS[k])
+        rows = pl.ds(OFFS[s][k], ROWS[s][k])
         step = min(half, 8)
 
         @pl.loop(0, half // step)
@@ -238,30 +249,59 @@
             else:
                 fin[at_, rows, :] = fin[at_, rows, :] + new
 
-    def core_add(k):
-        rows = pl.ds(OFFS[k], ROWS[k])
-
-        @pl.loop(0, 8)
-        def _(i):
-            at_ = pl.ds(i * 8, 8)
-            acc[core, at_, rows, :] = acc[core, at_, rows, :] + rc[at_, rows, :]
-
-    measure(0, 2)
-    for k in range(6):
-        core_copy(k).wait()
-        core_add(k)
-        round_copy(k, 0).start()
-    measure(2, 6)
-    for k in range(6):
-        round_copy(k, 0).wait()
-        round_add(k, 0)
-        round_copy(k, 1).start()
+    def core_add(s):
+        for k in range(6):
+            rows = pl.ds(OFFS[s][k], ROWS[s][k])
+            core_copy(s, k).wait()
+
+            @pl.loop(0, 4)
+            def _(i):
+                at_ = pl.ds(i * 16, 16)
+                acc[core, at_, rows, :] = acc[core, at_, rows, :] + rc[at_, rows, :]
+
+            round_copy(s, k, 0).start()
+
+    def advance(s, j):
+        for k in range(6):
+            round_copy(s, k, j).wait()
+            round_add(s, k, j)
+            round_copy(s, k, j + 1).start()
+
+    def finish(s):
+        for k in range(6):
+            round_copy(s, k, 5).wait()
+            place = base_of(k, 6)
+            for at_ in range(OFFS[s][k], OFFS[s][k] + ROWS[s][k], 16):
+                here = slice(at_, at_ + 16)
+                lanes = slice(at_ // 64 * 128, at_ // 64 * 128 + 128)
+                sblk[at_ % 64 : at_ % 64 + 16, lanes] = fin[place, here, :] + r5[0, here, :]
+
+    warp(0, TD, 0)
+    pl.semaphore_wait(barrier, NP - 1 + NV - 1)
+    combine(other, 0)
+    core_start(0)
+    gather_start(metag, 0)
+    combine(core, 0)
+    warp(0, 4, 1)
+    core_add(0)
+    warp(4, TD, 1)
+    combine(other, 1)
+    core_start(1)
+    combine(core, 1)
+    gather_wait(metag, 0)
+    measure(0, 1)
+    core_add(1)
+    advance(0, 0)
+    measure(1, 3)
+    advance(1, 0)
+    advance(0, 1)
+    measure(3, 6)
+    advance(1, 1)
+    advance(0, 2)
     measure(6, 8)
     gather_start(fluxg, 1)
-    for k in range(6):
-        round_copy(k, 1).wait()
-        round_add(k, 1)
-        round_copy(k, 2).start()
+    advance(1, 2)
+    advance(0, 3)
 
     own_row = source_lines(me, 16)
     own_col = source_lines(me, 20)
@@ -290,17 +330,11 @@
         mch[cols, :] = high
         mcl[cols, :] = low
 
-    for j in range(2, 5):
-        for k in range(6):
-            round_copy(k, j).wait()
-            round_add(k, j)
-            round_copy(k, j + 1).start()
-    for k in range(6):
-        round_copy(k, 5).wait()
-        place = base_of(k, 6)
-        for tile, first, count, to in PIECES[k]:
-            here = slice(OFFS[k] + to, OFFS[k] + to + count)
-            sblk[first : first + count, tile * 128 : tile * 128 + 128] = fin[place, here, :] + r5[0, here, :]
+    advance(1, 3)
+    advance(0, 4)
+    advance(1, 4)
+    finish(0)
+    finish(1)
 
     own = pl.ds(pl.multiple_of(v * 64, 64), 64)
     sg[own, :] = sblk[...].astype(BF16)
@@ -386,7 +420,7 @@
         resid_ref[t : t + 1, :] = fluxg[me, t : t + 1, :] - fits[t % 4] * template
 
 
-def fused(tile_patch, tile_weight, warped, match_rows, match_cols, src_row, src_col):
+def fused(tile_patch, tile_weight, images, warp_rows, warp_cols, match_rows, match_cols, src_row, src_col):
     dma = pltpu.SemaphoreType.DMA
     any_ = pl.BlockSpec(memory_space=pl.ANY)
     smem = pl.BlockSpec(memory_space=pltpu.SMEM)
@@ -398,9 +432,13 @@
             jax.ShapeDtypeStruct((4, 128), F32),
             jax.ShapeDtypeStruct((TD, S), F32),
         ),
-        in_specs=[smem, smem, any_, any_, any_, vmem, vmem],
+        in_specs=[smem, vmem, any_, any_, any_, any_, any_, vmem, vmem],
         out_specs=(vmem, vmem, vmem),
         scratch_shapes=[
+            pltpu.VMEM((TD, S, S), BF16),
+            pltpu.VMEM((TD, S, S), BF16),
+            pltpu.VMEM((TD, S, S), BF16),
+            pltpu.VMEM((2, S, 256), BF16),
             pltpu.VMEM((TD, S, S), BF16),
             pltpu.VMEM((S, S), F32),
             pltpu.VMEM((S, S), F32),
@@ -429,27 +467,22 @@
             pltpu.VMEM((64, S), F32),
             pltpu.SMEM((2 * NP,), jnp.int32),
             pltpu.SMEM((2 * NP,), F32),
-            dma((3,)), dma((6,)), dma((6,)), dma((6, 6)), dma((6, 6)),
+            pltpu.SMEM((TD,), F32),
+            dma((3, TD)), dma((3,)), dma((2, 6)), dma((2, 6)), dma((6, 12)), dma((6, 12)),
             dma((3, NP)), dma((3, NP)), dma((NV,)), dma((NV,)), dma((8,)), dma((8,)),
         ],
         compiler_params=pltpu.CompilerParams(
             collective_id=0, has_side_effects=True, vmem_limit_bytes=60 * 1024 * 1024
         ),
         name="coadd",
-    )(tile_patch, tile_weight, warped, match_rows, match_cols, src_row, src_col)
+    )(tile_patch, tile_weight, images, warp_rows, warp_cols, match_rows, match_cols, src_row, src_col)
 
 
 def shards(
     images, warp_rows, warp_cols, tile_weight, tile_patch, match_rows, match_cols, src_row, src_col
 ):
-    half_warp = jnp.einsum(
-        "tij,tkj->tik", images, warp_cols, preferred_element_type=jnp.float32
-    ).astype(jnp.bfloat16)
-    warped = jnp.einsum(
-        "tij,tjk->tik", warp_rows, half_warp, preferred_element_type=jnp.float32
-    ).astype(jnp.bfloat16)
     coadd, zero_point, resid = fused(
-        tile_patch, tile_weight.astype(F32), warped, match_rows[0], match_cols[0], src_row, src_col
+        tile_patch, tile_weight[None], images, warp_rows, warp_cols, match_rows[0], match_cols[0], src_row, src_col
     )
     return coadd[None], zero_point[:, 0], resid
 

time: 80.7 us -> 72.2 us (0.89)
  matrix products: 11.1 us -> 0 us
  Pallas kernels: 63.3 us -> 67.1 us
  other arithmetic: 1.17 us -> 0 us
    dot_general x1 -> x0, matrix products: 11.1 us -> none  [shards(): jnp.einsum('tij,tjk->tik', warp_rows, half_warp, preferred_element_type=j...]
    pallas_call x1, Pallas kernels: 63.3 us -> 67.1 us  [fused(): pl.pallas_call(kernel, out_shape=(jax.ShapeDtypeStruct((64, S), F32), jax...]
    convert_element_type x1 -> x0, other arithmetic: 1.17 us -> none  [shards(): tile_weight.astype(F32)]
where the time goes in v2:
time: 72.2 us; the launch traced here: 71.9 us
  Pallas kernels  67.1 us (93%)
  local copies, waits for them, and re-layouts  4.2 us (6%)
    pallas_call x1, Pallas kernels, fused(): pl.pallas_call(kernel, out_shape=(jax.ShapeDtypeStruct((64, S), F32), jax...  67.1 us
    unnamed x2, local copies, waits for them, and re-layouts  2.89 us

profile of v2, /device:TPU:1, one launch (start us, length us, event | category | flops | bytes accessed | tf_op | source)
XLA Modules:
  0.0 71.9 jit_solution(10824190171555259457)
XLA Ops:
  0.6 67.1 %coadd.1 = (f32[64,512]{1,0:T(8,128)}, f32[4,128]{1,0:T(4,128)}, f32[8,512]{1,0:T(8,128)}) custom-call(s32[8]{0:T(128)} %patch_sm.1, bf16[1,8]{1,0:T(2,128)(2,1)} %bitcast.7, bf16[8,512,512]{2,1,0:T(8,128)(2,1)} %img_hbm.1, bf16[8,512,512]{2,1,0:T(8,128)(2,1)} %wr_hbm.1, bf16[8,512,512]{2,1,0:T(8,128)(2,1)} %wc_hbm.1, f32[512,512]{1,0:T(8,128)} %bitcast.4, ...), custom_call_target="tpu_custom_call" | custom-call | tf_op jit(solution)/shard_map/coadd/pallas_call | solution.py:428
  67.7 1.3 %slice_reduce_fusion = f32[4]{0:T(128)} fusion(f32[4,128]{1,0:T(4,128)} %get-tuple-element.7), kind=kLoop, calls=%fused_computation | loop fusion | bytes 32 | tf_op jit(solution)/shard_map/slice | solution.py:487
  69.0 1.6 %copy.14 = f32[1,64,512]{2,1,0:T(8,128)} copy(f32[1,64,512]{2,1,0:T(8,128)} %bitcast.6) | data formatting | bytes 262144
  70.6 1.3 %copy.15 = f32[8,512]{1,0:T(8,128)} copy(f32[8,512]{1,0:T(8,128)} %get-tuple-element.14) | data formatting | bytes 32768

commit v3 on v2

--- a/solution.py
+++ b/solution.py
@@ -14,10 +14,7 @@
 MESH = pl.DeviceIdType.MESH
 
 ORDER = ("x0", "y0", "z0", "x1", "y1", "z1")
-ROWS = ((32, 32, 16, 16, 16, 16), (16, 16, 32, 32, 16, 16))
-OFFS = tuple(
-    tuple(s * 128 + sum(ROWS[s][:k]) for k in range(6)) for s in range(2)
-)
+UNITS = (((0, 1), (2, 3), (4,), (5,), (6,), (7,)), ((8,), (9,), (10, 11), (12, 13), (14,), (15,)))
 
 
 def gray(c):
@@ -50,9 +47,9 @@
 def kernel(
     patch_sm, weight_ref, img_hbm, wr_hbm, wc_hbm, mr_hbm, mc_hbm, srow_ref, scol_ref,
     coadd_ref, zp_ref, resid_ref,
-    img, wr, wc, halfs, warped, mr, mc, acc, rc, r0, r1, r2, fin, r3, r4, r5,
-    metag, fluxg, pg, refg, sg, colt, rowt, bth, btl, at, mch, mcl, mrow, sblk,
-    tab_i, tab_w, weight_sm, tsem, lsem, csem_s, csem_r, rsem_s, rsem_r, gsem_s, gsem_r, vsem_s, vsem_r, asem_s, asem_r,
+    img, wr, wc, halfs, warped, mr, mc, acc, rc, r0, r1, r2, fin,
+    metag, infog, fluxg, fluxo, pg, refg, sg, colt, rowt, bth, at, mch, mcl, sblk,
+    tab_i, tab_w, weight_sm, tsem, lsem, csem_s, csem_r, rsem_s, rsem_r, fsem_s, fsem_r, gsem_s, gsem_r, vsem_s, vsem_r, asem_s, asem_r,
 ):
     v = lax.axis_index("visit")
     me = lax.axis_index("patch")
@@ -85,6 +82,19 @@
     @pl.loop(1, NV)
     def _(o):
         pl.semaphore_signal(barrier, inc=1, device_id={"visit": (v + o) % NV, "patch": me}, device_id_type=MESH)
+
+    flips = {"x": (flip0(x), 3 - x), "y": (flip0(y), 3 - y), "z": (flip0(z), 3 - z)}
+    met = set()
+    for k in range(6):
+        last = tuple(sorted(ORDER[(k + 3 + i) % 6] for i in range(3)))
+        met |= {last, last[:2], (last[0], last[2])}
+    for dims in sorted(met):
+        where = {"x": x, "y": y, "z": z}
+        for d in dims:
+            where[d[0]] = flips[d[0]][int(d[1])]
+        there = {"visit": where["x"] * 2 + core, "patch": where["y"] * 4 + where["z"]}
+        pl.semaphore_signal(barrier, inc=1, device_id=there, device_id_type=MESH)
+    peers = NP - 1 + NV - 1 + len(met)
 
     def tile_load(i, t):
         hbm, buf = ((wc_hbm, wc), (img_hbm, img), (wr_hbm, wr))[i]
@@ -125,12 +135,12 @@
         tab_w[p] = wa
         tab_w[NP + p] = wb
 
+    low_lanes = lax.broadcasted_iota(jnp.int32, (1, 128), 1) < 64
     for t in range(TD):
-        metag[me, t : t + 1, :] = jnp.full((1, 128), patch_sm[t].astype(F32), F32)
-        metag[me, TD + t : TD + t + 1, :] = jnp.full((1, 128), weight_sm[t], F32)
+        infog[me, t : t + 1, :] = jnp.where(low_lanes, patch_sm[t].astype(F32), weight_sm[t])
     for c in range(4):
-        metag[me, 16 + c : 17 + c, :] = srow_ref[:, c * 128 : (c + 1) * 128].astype(F32)
-        metag[me, 20 + c : 21 + c, :] = scol_ref[:, c * 128 : (c + 1) * 128].astype(F32)
+        metag[me, c : 1 + c, :] = srow_ref[:, c * 128 : (c + 1) * 128].astype(F32)
+        metag[me, 4 + c : 5 + c, :] = scol_ref[:, c * 128 : (c + 1) * 128].astype(F32)
 
     def gather_copy(buf, kind, o):
         return remote(buf.at[me], buf.at[me], gsem_s.at[kind, o], gsem_r.at[kind, o], (v, (me + o) % NP))
@@ -146,20 +156,18 @@
             theirs = (me - o + NP) % NP
             remote(buf.at[theirs], buf.at[theirs], gsem_s.at[kind, o], gsem_r.at[kind, o], (v, (me + o) % NP)).wait()
 
-    def warp(first, last, s):
-        cols = slice(s * 256, s * 256 + 256)
-
-        @pl.loop(first // 2, last // 2)
+    def warp(first, last, step):
+        @pl.loop(first // step, last // step)
         def _(tt):
-            for i in range(2):
-                t = tt * 2 + i
-                if s == 0:
-                    for n in range(3):
-                        tile_load(n, t).wait()
-                halfs[i] = nt(img[t], wc[t, cols, :]).astype(BF16)
-            for i in range(2):
-                t = tt * 2 + i
-                warped[t, :, cols] = nn(wr[t], halfs[i]).astype(BF16)
+            for i in range(step):
+                t = tt * step + i
+                for n in range(2):
+                    tile_load(n, t).wait()
+                halfs[i] = nt(img[t], wc[t]).astype(BF16)
+            for i in range(step):
+                t = tt * step + i
+                tile_load(2, t).wait()
+                warped[t] = nn(wr[t], halfs[i]).astype(BF16)
 
     def combine(h, s):
         @pl.loop(0, NP)
@@ -176,16 +184,20 @@
                     place = 0
                     for j in range(6):
                         place = place * 2 + bits[ORDER[(k + j) % 6]]
-                    for at_ in range(OFFS[s][k], OFFS[s][k] + ROWS[s][k], 16):
-                        rows = pl.ds(pl.multiple_of((xr * 2 + h) * 64 + at_ % 64, 16), 16)
-                        lanes = slice(at_ // 64 * 128, at_ // 64 * 128 + 128)
-                        acc[h, place, at_ : at_ + 16, :] = (
+                    for i, unit in enumerate(UNITS[s][k]):
+                        rows = pl.ds(pl.multiple_of((xr * 2 + h) * 64 + unit % 4 * 16, 16), 16)
+                        lanes = slice(unit // 4 * 128, unit // 4 * 128 + 128)
+                        acc[h, UNITS[s][k][0] * 64 + place * len(UNITS[s][k]) + i] = (
                             warped[ia, rows, lanes] * wa + warped[ib, rows, lanes] * wb
                         )
 
+    def part(s, k, total, start, count):
+        n = len(UNITS[s][k])
+        return pl.ds(UNITS[s][k][0] * total + start * n, count * n)
+
     def core_copy(s, k):
-        rows = pl.ds(OFFS[s][k], ROWS[s][k])
-        return remote(acc.at[other, :, rows, :], rc.at[:, rows, :], csem_s.at[s, k], csem_r.at[s, k], mate)
+        span = part(s, k, 64, 0, 64)
+        return remote(acc.at[other, span], rc.at[span], csem_s.at[s, k], csem_r.at[s, k], mate)
 
     def core_start(s):
         for k in range(6):
@@ -198,8 +210,8 @@
         @pl.loop(first, last)
         def _(t):
             q = patch_sm[t]
-            row_of = source_lines(q, 16)
-            col_of = source_lines(q, 20)
+            row_of = source_lines(q, 0)
+            col_of = source_lines(q, 4)
 
             @pl.loop(0, 4)
             def _(b):
@@ -213,14 +225,13 @@
                 return total + jnp.sum((by_col * rows).reshape(16, 8, S), axis=0)
 
             total = lax.fori_loop(0, 4, part, jnp.zeros((8, S), F32))
-            fluxg[me, pl.ds(t, 1), :] = jnp.sum(total, axis=0, keepdims=True)
-
-    bufs = (r0, r1, r2, r3, r4, r5)
+            fluxo[pl.ds(t, 1), :] = jnp.sum(total, axis=0, keepdims=True)
+
+    bufs = (r0, r1, r2)
 
     def base_of(k, j):
-        lo = 0 if j < 3 else 3
         base = 0
-        for i in range(lo, j):
+        for i in range(j):
             base = base + side[ORDER[(k + i) % 6]] * (32 >> i)
         return base
 
@@ -228,36 +239,44 @@
         d = ORDER[(k + j) % 6]
         half = 32 >> j
         start = base_of(k, j) + (1 - side[d]) * half
-        rows = pl.ds(OFFS[s][k], ROWS[s][k])
-        src = acc.at[core, pl.ds(start, half), rows, :] if j < 3 else fin.at[pl.ds(start, half), rows, :]
-        return remote(src, bufs[j].at[:, rows, :], rsem_s.at[j, s * 6 + k], rsem_r.at[j, s * 6 + k], partner[d])
+        src = acc.at[core, part(s, k, 64, start, half)]
+        dst = bufs[j].at[part(s, k, half, 0, half)]
+        return remote(src, dst, rsem_s.at[j, s * 6 + k], rsem_r.at[j, s * 6 + k], partner[d])
 
     def round_add(s, k, j):
         half = 32 >> j
-        keep = base_of(k, j + 1) if j != 2 else base_of(k, 2) + side[ORDER[(k + 2) % 6]] * half
-        rows = pl.ds(OFFS[s][k], ROWS[s][k])
-        step = min(half, 8)
+        step = min(half, 16)
 
         @pl.loop(0, half // step)
         def _(i):
-            new = bufs[j][pl.ds(i * step, step), rows, :]
-            at_ = pl.ds(keep + i * step, step)
-            if j < 2:
-                acc[core, at_, rows, :] = acc[core, at_, rows, :] + new
-            elif j == 2:
-                fin[pl.ds(i * step, step), rows, :] = acc[core, at_, rows, :].astype(F32) + new.astype(F32)
-            else:
-                fin[at_, rows, :] = fin[at_, rows, :] + new
+            at_ = part(s, k, 64, base_of(k, j + 1) + i * step, step)
+            acc[core, at_] = acc[core, at_] + bufs[j][part(s, k, half, i * step, step)]
+
+    def last_copy(s, k, e):
+        place = base_of(k, 3)
+        where = {"x": x, "y": y, "z": z}
+        for i in range(3):
+            d = ORDER[(k + 3 + i) % 6]
+            bit = side[d]
+            if e >> (2 - i) & 1:
+                bit = 1 - bit
+                c = where[d[0]]
+                where[d[0]] = flip0(c) if d[1] == "0" else 3 - c
+            place = place + bit * (4 >> i)
+        there = (where["x"] * 2 + core, where["y"] * 4 + where["z"])
+        return remote(
+            acc.at[core, part(s, k, 64, place, 1)], fin.at[part(s, k, 8, e, 1)],
+            fsem_s.at[s * 6 + k, e], fsem_r.at[s * 6 + k, e], there,
+        )
 
     def core_add(s):
         for k in range(6):
-            rows = pl.ds(OFFS[s][k], ROWS[s][k])
             core_copy(s, k).wait()
 
             @pl.loop(0, 4)
             def _(i):
-                at_ = pl.ds(i * 16, 16)
-                acc[core, at_, rows, :] = acc[core, at_, rows, :] + rc[at_, rows, :]
+                at_ = part(s, k, 64, i * 16, 16)
+                acc[core, at_] = acc[core, at_] + rc[at_]
 
             round_copy(s, k, 0).start()
 
@@ -265,46 +284,52 @@
         for k in range(6):
             round_copy(s, k, j).wait()
             round_add(s, k, j)
-            round_copy(s, k, j + 1).start()
+            if j < 2:
+                round_copy(s, k, j + 1).start()
+            else:
+                for e in (7, 6, 5, 3, 4, 2, 1):
+                    last_copy(s, k, e).start()
 
     def finish(s):
         for k in range(6):
-            round_copy(s, k, 5).wait()
+            n = len(UNITS[s][k])
             place = base_of(k, 6)
-            for at_ in range(OFFS[s][k], OFFS[s][k] + ROWS[s][k], 16):
-                here = slice(at_, at_ + 16)
-                lanes = slice(at_ // 64 * 128, at_ // 64 * 128 + 128)
-                sblk[at_ % 64 : at_ % 64 + 16, lanes] = fin[place, here, :] + r5[0, here, :]
-
-    warp(0, TD, 0)
-    pl.semaphore_wait(barrier, NP - 1 + NV - 1)
+            for e in (1, 2, 4, 3, 5, 6, 7):
+                last_copy(s, k, e).wait()
+            for i, unit in enumerate(UNITS[s][k]):
+                value = acc[core, UNITS[s][k][0] * 64 + place * n + i].astype(F32)
+                for e in range(1, 8):
+                    value = value + fin[UNITS[s][k][0] * 8 + e * n + i].astype(F32)
+                lanes = slice(unit // 4 * 128, unit // 4 * 128 + 128)
+                sblk[unit % 4 * 16 : unit % 4 * 16 + 16, lanes] = value
+
+    warp(0, 6, 2)
+    warp(6, TD, 1)
+    pl.semaphore_wait(barrier, peers)
     combine(other, 0)
     core_start(0)
     gather_start(metag, 0)
-    combine(core, 0)
-    warp(0, 4, 1)
-    core_add(0)
-    warp(4, TD, 1)
     combine(other, 1)
     core_start(1)
+    combine(core, 0)
     combine(core, 1)
+    core_add(0)
+    core_add(1)
     gather_wait(metag, 0)
-    measure(0, 1)
-    core_add(1)
+    measure(0, 2)
     advance(0, 0)
-    measure(1, 3)
+    measure(2, 4)
     advance(1, 0)
+    measure(4, 6)
     advance(0, 1)
-    measure(3, 6)
     advance(1, 1)
+    measure(6, 8)
+    fluxg[me] = fluxo[...].astype(BF16)
     advance(0, 2)
-    measure(6, 8)
-    gather_start(fluxg, 1)
-    advance(1, 2)
-    advance(0, 3)
-
-    own_row = source_lines(me, 16)
-    own_col = source_lines(me, 20)
+    gather_start(infog, 3)
+
+    own_row = source_lines(me, 0)
+    own_col = source_lines(me, 4)
 
     @pl.loop(0, 4)
     def _(b):
@@ -321,18 +346,20 @@
         cols = pl.ds(start, 128)
         high, low = split(mc[:, cols])
         value = tn(high, colt[...]) + tn(low, colt[...])
-        high, low = split(value)
-        bth[cols, :] = high
-        btl[cols, :] = low
+        bth[cols, :] = value.astype(BF16)
         high, low = split(mr[:, cols])
         at[cols, :] = tn(high, rowt[...]) + tn(low, rowt[...])
         high, low = split(mc[cols, :])
         mch[cols, :] = high
         mcl[cols, :] = low
 
-    advance(1, 3)
-    advance(0, 4)
-    advance(1, 4)
+    advance(1, 2)
+    gather_start(fluxg, 1)
+    gather_wait(infog, 3)
+    info = infog[...].reshape(128, 128)
+    mine = (info == me.astype(F32)) & (lax.broadcasted_iota(jnp.int32, (128, 128), 1) < 64)
+    weights = jnp.where(mine, pltpu.roll(info, 64, 1), 0.0)
+    weight_sum = jnp.sum(jnp.sum(weights, axis=0, keepdims=True), axis=1, keepdims=True) * (1.0 / 64.0)
     finish(0)
     finish(1)
 
@@ -352,13 +379,12 @@
         return remote(sg.at[rows, :], sg.at[rows, :], asem_s.at[3 + o], asem_r.at[3 + o], mate)
 
     high, low = split(sblk[...])
-    value = nn(high, bth[...]) + nn(low, bth[...]) + nn(high, btl[...])
+    value = nn(jnp.concatenate([high, low], axis=0), bth[...])
+    value = value[0:64] + value[64:128]
     partial = jnp.sum(value * at[own, :], axis=0, keepdims=True)
     for c in range(4):
         pg[v, c : c + 1, :] = partial[:, c * 128 : (c + 1) * 128]
-    mine = metag[:, 0:8, :].reshape(128, 128) == me.astype(F32)
-    weights = jnp.where(mine, metag[:, 8:16, :].reshape(128, 128), 0.0)
-    pg[v, 4:5, :] = jnp.sum(weights, axis=0, keepdims=True)
+    pg[v, 4:5, :] = jnp.broadcast_to(weight_sum, (1, 128))
     pg[v, 5:8, :] = jnp.zeros((3, 128), F32)
 
     @pl.loop(1, NV)
@@ -371,10 +397,9 @@
     gather_wait(fluxg, 1)
     tile = lax.broadcasted_iota(jnp.int32, (128, 128), 0)
     lane = lax.broadcasted_iota(jnp.int32, (128, 128), 1)
-    hits = (metag[:, 0:8, :].reshape(128, 128) == (lane % 16).astype(F32)) & (tile % 4 == lane // 16)
+    hits = (infog[...].reshape(128, 128) == (lane % 16).astype(F32)) & (tile % 4 == lane // 16)
     hits = jnp.where(hits, 1.0, 0.0).astype(BF16)
-    high, low = split(fluxg[...].reshape(128, S))
-    sums = tn(hits, high) + tn(hits, low)
+    sums = tn(hits, fluxg[...].reshape(128, S))
     counts = tn(hits, jnp.ones((128, 128), BF16))
 
     @pl.loop(1, NV)
@@ -417,7 +442,7 @@
     for t in range(TD):
         q = patch_sm[t]
         template = jnp.concatenate([refg[q, c : c + 1, :] for c in range(4)], axis=1)
-        resid_ref[t : t + 1, :] = fluxg[me, t : t + 1, :] - fits[t % 4] * template
+        resid_ref[t : t + 1, :] = fluxo[t : t + 1, :] - fits[t % 4] * template
 
 
 def fused(tile_patch, tile_weight, images, warp_rows, warp_cols, match_rows, match_cols, src_row, src_col):
@@ -438,24 +463,22 @@
             pltpu.VMEM((TD, S, S), BF16),
             pltpu.VMEM((TD, S, S), BF16),
             pltpu.VMEM((TD, S, S), BF16),
-            pltpu.VMEM((2, S, 256), BF16),
+            pltpu.VMEM((2, S, S), BF16),
             pltpu.VMEM((TD, S, S), BF16),
             pltpu.VMEM((S, S), F32),
             pltpu.VMEM((S, S), F32),
-            pltpu.VMEM((2, 64, 256, 128), BF16),
-            pltpu.VMEM((64, 256, 128), BF16),
-            pltpu.VMEM((32, 256, 128), BF16),
-            pltpu.VMEM((16, 256, 128), BF16),
-            pltpu.VMEM((8, 256, 128), BF16),
-            pltpu.VMEM((8, 256, 128), F32),
-            pltpu.VMEM((4, 256, 128), F32),
-            pltpu.VMEM((2, 256, 128), F32),
-            pltpu.VMEM((1, 256, 128), F32),
-            pltpu.VMEM((NP, 24, 128), F32),
-            pltpu.VMEM((NP, TD, S), F32),
+            pltpu.VMEM((2, 64 * 16, 16, 128), BF16),
+            pltpu.VMEM((64 * 16, 16, 128), BF16),
+            pltpu.VMEM((32 * 16, 16, 128), BF16),
+            pltpu.VMEM((16 * 16, 16, 128), BF16),
+            pltpu.VMEM((8 * 16, 16, 128), BF16),
+            pltpu.VMEM((8 * 16, 16, 128), BF16),
+            pltpu.VMEM((NP, 8, 128), F32),
+            pltpu.VMEM((NP, TD, 128), F32),
+            pltpu.VMEM((NP, TD, S), BF16),
+            pltpu.VMEM((TD, S), F32),
             pltpu.VMEM((NV, 8, 128), F32),
             pltpu.VMEM((NP, 8, 128), F32),
-            pltpu.VMEM((S, S), BF16),
             pltpu.VMEM((S, S), BF16),
             pltpu.VMEM((S, S), BF16),
             pltpu.VMEM((S, S), BF16),
@@ -464,12 +487,11 @@
             pltpu.VMEM((S, S), BF16),
             pltpu.VMEM((S, S), BF16),
             pltpu.VMEM((64, S), F32),
-            pltpu.VMEM((64, S), F32),
             pltpu.SMEM((2 * NP,), jnp.int32),
             pltpu.SMEM((2 * NP,), F32),
             pltpu.SMEM((TD,), F32),
-            dma((3, TD)), dma((3,)), dma((2, 6)), dma((2, 6)), dma((6, 12)), dma((6, 12)),
-            dma((3, NP)), dma((3, NP)), dma((NV,)), dma((NV,)), dma((8,)), dma((8,)),
+            dma((3, TD)), dma((3,)), dma((2, 6)), dma((2, 6)), dma((3, 12)), dma((3, 12)), dma((12, 8)), dma((12, 8)),
+            dma((4, NP)), dma((4, NP)), dma((NV,)), dma((NV,)), dma((8,)), dma((8,)),
         ],
         compiler_params=pltpu.CompilerParams(
             collective_id=0, has_side_effects=True, vmem_limit_bytes=60 * 1024 * 1024
@@ -478,13 +500,31 @@
     )(tile_patch, tile_weight, images, warp_rows, warp_cols, match_rows, match_cols, src_row, src_col)
 
 
+def store(coadd_in, zp_in, resid_in, coadd_ref, zp_ref, resid_ref):
+    coadd_ref[0] = coadd_in[...]
+    resid_ref[...] = resid_in[...]
+    for u in range(4):
+        zp_ref[u] = jnp.max(zp_in[u : u + 1, :])
+
+
 def shards(
     images, warp_rows, warp_cols, tile_weight, tile_patch, match_rows, match_cols, src_row, src_col
 ):
     coadd, zero_point, resid = fused(
         tile_patch, tile_weight[None], images, warp_rows, warp_cols, match_rows[0], match_cols[0], src_row, src_col
     )
-    return coadd[None], zero_point[:, 0], resid
+    vmem = pl.BlockSpec(memory_space=pltpu.VMEM)
+    return pl.pallas_call(
+        store,
+        out_shape=(
+            jax.ShapeDtypeStruct((1, 64, S), F32),
+            jax.ShapeDtypeStruct((4,), F32),
+            jax.ShapeDtypeStruct((TD, S), F32),
+        ),
+        in_specs=[vmem, vmem, vmem],
+        out_specs=(vmem, pl.BlockSpec(memory_space=pltpu.SMEM), vmem),
+        name="store",
+    )(coadd, zero_point, resid)
 
 
 def solution(mesh):

time: 72.2 us -> 65.2 us (0.903)
  local copies, waits for them, and re-layouts: 4.2 us -> 0 us
  Pallas kernels: 67.1 us -> 64.4 us
    pallas_call x1, Pallas kernels: 67.1 us -> 62.8 us  [fused(): pl.pallas_call(kernel, out_shape=(jax.ShapeDtypeStruct((64, S), F32), jax...]
    unnamed x2 -> x0, local copies, waits for them, and re-layouts: 2.89 us -> none
    pallas_call x0 -> x1, Pallas kernels: none -> 1.59 us  [shards(): pl.pallas_call(store, out_shape=(jax.ShapeDtypeStruct((1, 64, S), F32), j...]
    slice x1 -> x0, local copies, waits for them, and re-layouts: 1.31 us -> none  [shards(): return (coadd[None], zero_point[:, 0], resid)]
where the time goes in v3:
time: 65.2 us; the launch traced here: 65 us
  Pallas kernels  64.4 us (99%)
    pallas_call x1, Pallas kernels, fused(): pl.pallas_call(kernel, out_shape=(jax.ShapeDtypeStruct((64, S), F32), jax...  62.8 us
    pallas_call x1, Pallas kernels, shards(): pl.pallas_call(store, out_shape=(jax.ShapeDtypeStruct((1, 64, S), F32), j...  1.59 us

profile of v3, /device:TPU:1, one launch (start us, length us, event | category | flops | bytes accessed | tf_op | source)
XLA Modules:
  0.0 65.0 jit_solution(11183261197962282224)
XLA Ops:
  0.6 62.8 %coadd.1 = (f32[64,512]{1,0:T(8,128)}, f32[4,128]{1,0:T(4,128)}, f32[8,512]{1,0:T(8,128)}) custom-call(s32[8]{0:T(128)} %patch_sm.1, bf16[1,8]{1,0:T(2,128)(2,1)} %bitcast.5, bf16[8,512,512]{2,1,0:T(8,128)(2,1)} %img_hbm.1, bf16[8,512,512]{2,1,0:T(8,128)(2,1)} %wr_hbm.1, bf16[8,512,512]{2,1,0:T(8,128)(2,1)} %wc_hbm.1, f32[512,512]{1,0:T(8,128)} %bitcast.3, ...), custom_call_target="tpu_custom_call" | custom-call | tf_op jit(solution)/shard_map/coadd/pallas_call | solution.py:453
  63.4 1.6 %store.1 = (f32[1,64,512]{2,1,0:T(8,128)}, f32[4]{0:T(128)}, f32[8,512]{1,0:T(8,128)}) custom-call(f32[64,512]{1,0:T(8,128)} %get-tuple-element.6.coadd_in, f32[4,128]{1,0:T(4,128)} %get-tuple-element.7.zp_in, f32[8,512]{1,0:T(8,128)} %get-tuple-element.8.resid_in), custom_call_target="tpu_custom_call" | custom-call | tf_op jit(solution)/shard_map/store/pallas_call | solution.py:517

commit v4 on v3

--- a/solution.py
+++ b/solution.py
@@ -47,7 +47,7 @@
 def kernel(
     patch_sm, weight_ref, img_hbm, wr_hbm, wc_hbm, mr_hbm, mc_hbm, srow_ref, scol_ref,
     coadd_ref, zp_ref, resid_ref,
-    img, wr, wc, halfs, warped, mr, mc, acc, rc, r0, r1, r2, fin,
+    img, wr, wc, halfs, warped, mr, mc, acc, rc, r0, r1, r2, fin, sums, counts, value,
     metag, infog, fluxg, fluxo, pg, refg, sg, colt, rowt, bth, at, mch, mcl, sblk,
     tab_i, tab_w, weight_sm, tsem, lsem, csem_s, csem_r, rsem_s, rsem_r, fsem_s, fsem_r, gsem_s, gsem_r, vsem_s, vsem_r, asem_s, asem_r,
 ):
@@ -106,9 +106,7 @@
             tile_load(i, t).start()
 
     load_r = pltpu.make_async_copy(mr_hbm, mr, lsem.at[1])
-    load_r.start()
     load_c = pltpu.make_async_copy(mc_hbm, mc, lsem.at[2])
-    load_c.start()
 
     lane8 = lax.broadcasted_iota(jnp.int32, (1, TD), 1)
     for t in range(TD):
@@ -303,6 +301,70 @@
                 lanes = slice(unit // 4 * 128, unit // 4 * 128 + 128)
                 sblk[unit % 4 * 16 : unit % 4 * 16 + 16, lanes] = value
 
+    def tables():
+        own_row = source_lines(me, 0)
+        own_col = source_lines(me, 4)
+
+        @pl.loop(0, 4)
+        def _(b):
+            start = pl.multiple_of(b * 128, 128)
+            colt[pl.ds(start, 128), :] = profile(own_col, (b * 128).astype(F32), 128)
+            rowt[pl.ds(start, 128), :] = profile(own_row, (b * 128).astype(F32), 128)
+
+        load_r.wait()
+        load_c.wait()
+
+        @pl.loop(0, 4)
+        def _(b):
+            start = pl.multiple_of(b * 128, 128)
+            cols = pl.ds(start, 128)
+            high, low = split(mc[:, cols])
+            value = tn(high, colt[...]) + tn(low, colt[...])
+            bth[cols, :] = value.astype(BF16)
+            high, low = split(mr[:, cols])
+            at[cols, :] = tn(high, rowt[...]) + tn(low, rowt[...])
+            high, low = split(mc[cols, :])
+            mch[cols, :] = high
+            mcl[cols, :] = low
+
+    def rows_of(who):
+        return pl.ds(pl.multiple_of(who * 64, 64), 64)
+
+    own = rows_of(v)
+
+    def share_copy(s, o):
+        src = sg.at[s, own, :]
+        where = mate if o == 0 else (((x + o) % 4) * 2 + core, me)
+        return remote(src, src, asem_s.at[s, o], asem_r.at[s, o], where)
+
+    def share_start(s):
+        sg[s, own, :] = sblk[:, s * 256 : s * 256 + 256].astype(BF16)
+        for o in (2, 1, 3, 0):
+            share_copy(s, o).start()
+
+    def came(s, o, base, half):
+        rows = rows_of(((x - o + 4) % 4) * 2 + half)
+        block = sg.at[s, rows, :]
+        where = (((x + o) % 4) * 2 + core, me) if base == 0 else mate
+        return remote(block, block, asem_s.at[s, base + o], asem_r.at[s, base + o], where)
+
+    def share_pass(s):
+        for o in (1, 3, 2):
+            came(s, o, 0, core).wait()
+            block = sg.at[s, rows_of(((x - o + 4) % 4) * 2 + core), :]
+            remote(block, block, asem_s.at[s, 4 + o], asem_r.at[s, 4 + o], mate).start()
+
+    def share_end(s):
+        came(s, 0, 0, other).wait()
+        for o in (1, 3, 2):
+            came(s, o, 4, other).wait()
+
+    def own_flux(s):
+        cols = slice(s * 256, s * 256 + 256)
+        high, low = split(sblk[:, cols])
+        value = nn(jnp.concatenate([high, low], axis=0), bth[cols, :])
+        return value[0:64] + value[64:128]
+
     warp(0, 6, 2)
     warp(6, TD, 1)
     pl.semaphore_wait(barrier, peers)
@@ -311,9 +373,11 @@
     gather_start(metag, 0)
     combine(other, 1)
     core_start(1)
+    load_r.start()
+    load_c.start()
     combine(core, 0)
+    core_add(0)
     combine(core, 1)
-    core_add(0)
     core_add(1)
     gather_wait(metag, 0)
     measure(0, 2)
@@ -322,85 +386,44 @@
     advance(1, 0)
     measure(4, 6)
     advance(0, 1)
+    gather_start(infog, 3)
+    measure(6, 7)
     advance(1, 1)
-    measure(6, 8)
+    measure(7, 8)
     fluxg[me] = fluxo[...].astype(BF16)
+    tables()
     advance(0, 2)
-    gather_start(infog, 3)
-
-    own_row = source_lines(me, 0)
-    own_col = source_lines(me, 4)
-
-    @pl.loop(0, 4)
-    def _(b):
-        start = pl.multiple_of(b * 128, 128)
-        colt[pl.ds(start, 128), :] = profile(own_col, (b * 128).astype(F32), 128)
-        rowt[pl.ds(start, 128), :] = profile(own_row, (b * 128).astype(F32), 128)
-
-    load_r.wait()
-    load_c.wait()
-
-    @pl.loop(0, 4)
-    def _(b):
-        start = pl.multiple_of(b * 128, 128)
-        cols = pl.ds(start, 128)
-        high, low = split(mc[:, cols])
-        value = tn(high, colt[...]) + tn(low, colt[...])
-        bth[cols, :] = value.astype(BF16)
-        high, low = split(mr[:, cols])
-        at[cols, :] = tn(high, rowt[...]) + tn(low, rowt[...])
-        high, low = split(mc[cols, :])
-        mch[cols, :] = high
-        mcl[cols, :] = low
-
-    advance(1, 2)
-    gather_start(fluxg, 1)
     gather_wait(infog, 3)
     info = infog[...].reshape(128, 128)
     mine = (info == me.astype(F32)) & (lax.broadcasted_iota(jnp.int32, (128, 128), 1) < 64)
     weights = jnp.where(mine, pltpu.roll(info, 64, 1), 0.0)
     weight_sum = jnp.sum(jnp.sum(weights, axis=0, keepdims=True), axis=1, keepdims=True) * (1.0 / 64.0)
+    pg[v, 4:5, :] = jnp.broadcast_to(weight_sum, (1, 128))
+    pg[v, 5:8, :] = jnp.zeros((3, 128), F32)
+    advance(1, 2)
+
+    gather_start(fluxg, 1)
     finish(0)
+    share_start(0)
+    value[...] = own_flux(0)
     finish(1)
-
-    own = pl.ds(pl.multiple_of(v * 64, 64), 64)
-    sg[own, :] = sblk[...].astype(BF16)
-
-    def rows_of(who):
-        return pl.ds(pl.multiple_of(who * 64, 64), 64)
-
-    def share_copy(o):
-        if o == 0:
-            return remote(sg.at[own, :], sg.at[own, :], asem_s.at[0], asem_r.at[0], mate)
-        return remote(sg.at[own, :], sg.at[own, :], asem_s.at[o], asem_r.at[o], (((x + o) % 4) * 2 + core, me))
-
-    def pass_copy(o):
-        rows = rows_of(((x - o + 4) % 4) * 2 + core)
-        return remote(sg.at[rows, :], sg.at[rows, :], asem_s.at[3 + o], asem_r.at[3 + o], mate)
-
-    high, low = split(sblk[...])
-    value = nn(jnp.concatenate([high, low], axis=0), bth[...])
-    value = value[0:64] + value[64:128]
-    partial = jnp.sum(value * at[own, :], axis=0, keepdims=True)
+    share_start(1)
+    partial = jnp.sum((value[...] + own_flux(1)) * at[own, :], axis=0, keepdims=True)
     for c in range(4):
         pg[v, c : c + 1, :] = partial[:, c * 128 : (c + 1) * 128]
-    pg[v, 4:5, :] = jnp.broadcast_to(weight_sum, (1, 128))
-    pg[v, 5:8, :] = jnp.zeros((3, 128), F32)
 
     @pl.loop(1, NV)
     def _(o):
         remote(pg.at[v], pg.at[v], vsem_s.at[o], vsem_r.at[o], ((v + o) % NV, me)).start()
 
-    for o in (1, 3, 2, 0):
-        share_copy(o).start()
-
+    share_pass(0)
     gather_wait(fluxg, 1)
     tile = lax.broadcasted_iota(jnp.int32, (128, 128), 0)
     lane = lax.broadcasted_iota(jnp.int32, (128, 128), 1)
     hits = (infog[...].reshape(128, 128) == (lane % 16).astype(F32)) & (tile % 4 == lane // 16)
     hits = jnp.where(hits, 1.0, 0.0).astype(BF16)
-    sums = tn(hits, fluxg[...].reshape(128, S))
-    counts = tn(hits, jnp.ones((128, 128), BF16))
+    sums[...] = tn(hits, fluxg[...].reshape(128, S))
+    counts[...] = tn(hits, jnp.ones((128, 128), BF16))
 
     @pl.loop(1, NV)
     def _(o):
@@ -412,19 +435,17 @@
     refg[me] = total * inverse
     gather_start(refg, 2)
 
-    for o in (1, 3, 2):
-        rows = rows_of(((x - o + 4) % 4) * 2 + core)
-        remote(sg.at[rows, :], sg.at[rows, :], asem_s.at[o], asem_r.at[o], (((x + o) % 4) * 2 + core, me)).wait()
-        pass_copy(o).start()
-    mates = rows_of(x * 2 + other)
-    remote(sg.at[mates, :], sg.at[mates, :], asem_s.at[0], asem_r.at[0], mate).wait()
-    for o in (1, 3, 2):
-        rows = rows_of(((x - o + 4) % 4) * 2 + other)
-        remote(sg.at[rows, :], sg.at[rows, :], asem_s.at[3 + o], asem_r.at[3 + o], mate).wait()
-    high, low = split(mr[own, :])
-    matched = nn(high, sg[...]) + nn(low, sg[...])
-    high, low = split(matched)
-    matched = nt(high, mch[...]) + nt(low, mch[...]) + nt(high, mcl[...])
+    share_pass(1)
+    mrow_high, mrow_low = split(mr[own, :])
+    both = jnp.concatenate([mrow_high, mrow_low], axis=0)
+    matched = jnp.zeros((64, S), F32)
+    for s in range(2):
+        share_end(s)
+        cols = slice(s * 256, s * 256 + 256)
+        half = nn(both, sg[s])
+        high, low = split(half[0:64] + half[64:128])
+        pair = nt(jnp.concatenate([high, low], axis=0), mch[:, cols])
+        matched = matched + pair[0:64] + pair[64:128] + nt(high, mcl[:, cols])
     for c in range(4):
         coadd_ref[:, c * 128 : (c + 1) * 128] = matched[:, c * 128 : (c + 1) * 128] * inverse
 
@@ -473,13 +494,16 @@
             pltpu.VMEM((16 * 16, 16, 128), BF16),
             pltpu.VMEM((8 * 16, 16, 128), BF16),
             pltpu.VMEM((8 * 16, 16, 128), BF16),
+            pltpu.VMEM((128, S), F32),
+            pltpu.VMEM((128, 128), F32),
+            pltpu.VMEM((64, S), F32),
             pltpu.VMEM((NP, 8, 128), F32),
             pltpu.VMEM((NP, TD, 128), F32),
             pltpu.VMEM((NP, TD, S), BF16),
             pltpu.VMEM((TD, S), F32),
             pltpu.VMEM((NV, 8, 128), F32),
             pltpu.VMEM((NP, 8, 128), F32),
-            pltpu.VMEM((S, S), BF16),
+            pltpu.VMEM((2, S, 256), BF16),
             pltpu.VMEM((S, S), BF16),
             pltpu.VMEM((S, S), BF16),
             pltpu.VMEM((S, S), BF16),
@@ -491,7 +515,7 @@
             pltpu.SMEM((2 * NP,), F32),
             pltpu.SMEM((TD,), F32),
             dma((3, TD)), dma((3,)), dma((2, 6)), dma((2, 6)), dma((3, 12)), dma((3, 12)), dma((12, 8)), dma((12, 8)),
-            dma((4, NP)), dma((4, NP)), dma((NV,)), dma((NV,)), dma((8,)), dma((8,)),
+            dma((4, NP)), dma((4, NP)), dma((NV,)), dma((NV,)), dma((2, 8)), dma((2, 8)),
         ],
         compiler_params=pltpu.CompilerParams(
             collective_id=0, has_side_effects=True, vmem_limit_bytes=60 * 1024 * 1024

time: 65.2 us -> 62.7 us (0.962)
  Pallas kernels: 64.4 us -> 61.9 us
    pallas_call x1, Pallas kernels: 62.8 us -> 60.3 us  [fused(): pl.pallas_call(kernel, out_shape=(jax.ShapeDtypeStruct((64, S), F32), jax...]
where the time goes in v4:
time: 62.7 us; the launch traced here: 62.5 us
  Pallas kernels  61.9 us (99%)
  between operations  0.64 us (1%)
    pallas_call x1, Pallas kernels, fused(): pl.pallas_call(kernel, out_shape=(jax.ShapeDtypeStruct((64, S), F32), jax...  60.3 us
    pallas_call x1, Pallas kernels, shards(): pl.pallas_call(store, out_shape=(jax.ShapeDtypeStruct((1, 64, S), F32), j...  1.59 us

profile of v4, /device:TPU:1, one launch (start us, length us, event | category | flops | bytes accessed | tf_op | source)
XLA Modules:
  0.0 62.5 jit_solution(9783409543346518606)
XLA Ops:
  0.6 60.3 %coadd.1 = (f32[64,512]{1,0:T(8,128)}, f32[4,128]{1,0:T(4,128)}, f32[8,512]{1,0:T(8,128)}) custom-call(s32[8]{0:T(128)} %patch_sm.1, bf16[1,8]{1,0:T(2,128)(2,1)} %bitcast.5, bf16[8,512,512]{2,1,0:T(8,128)(2,1)} %img_hbm.1, bf16[8,512,512]{2,1,0:T(8,128)(2,1)} %wr_hbm.1, bf16[8,512,512]{2,1,0:T(8,128)(2,1)} %wc_hbm.1, f32[512,512]{1,0:T(8,128)} %bitcast.3, ...), custom_call_target="tpu_custom_call" | custom-call | tf_op jit(solution)/shard_map/coadd/pallas_call | solution.py:474
  60.9 1.6 %store.1 = (f32[1,64,512]{2,1,0:T(8,128)}, f32[4]{0:T(128)}, f32[8,512]{1,0:T(8,128)}) custom-call(f32[64,512]{1,0:T(8,128)} %get-tuple-element.6.coadd_in, f32[4,128]{1,0:T(4,128)} %get-tuple-element.7.zp_in, f32[8,512]{1,0:T(8,128)} %get-tuple-element.8.resid_in), custom_call_target="tpu_custom_call" | custom-call | tf_op jit(solution)/shard_map/store/pallas_call | solution.py:541

commit v5 on v4

--- a/solution.py
+++ b/solution.py
@@ -14,7 +14,7 @@
 MESH = pl.DeviceIdType.MESH
 
 ORDER = ("x0", "y0", "z0", "x1", "y1", "z1")
-UNITS = (((0, 1), (2, 3), (4,), (5,), (6,), (7,)), ((8,), (9,), (10, 11), (12, 13), (14,), (15,)))
+UNITS = (((0, 1), (2, 3), (4, 5), (6, 7), (8,), (9,)), ((10,), (11,), (12,), (13,), (14,), (15,)))
 
 
 def gray(c):
@@ -176,16 +176,26 @@
             bits = {}
             bits["y1"], bits["y0"] = gray(p // 4)
             bits["z1"], bits["z0"] = gray(p % 4)
+            starts = []
+            for k in range(6):
+                place = 0
+                for j in range(6):
+                    d = ORDER[(k + j) % 6]
+                    if d[0] != "x":
+                        place = place + bits[d] * (32 >> j)
+                starts.append(place * len(UNITS[s][k]) + UNITS[s][k][0] * 64)
             for xr in range(4):
                 bits["x1"], bits["x0"] = gray(xr)
                 for k in range(6):
-                    place = 0
+                    shift = 0
                     for j in range(6):
-                        place = place * 2 + bits[ORDER[(k + j) % 6]]
+                        d = ORDER[(k + j) % 6]
+                        if d[0] == "x":
+                            shift += bits[d] * (32 >> j)
                     for i, unit in enumerate(UNITS[s][k]):
                         rows = pl.ds(pl.multiple_of((xr * 2 + h) * 64 + unit % 4 * 16, 16), 16)
                         lanes = slice(unit // 4 * 128, unit // 4 * 128 + 128)
-                        acc[h, UNITS[s][k][0] * 64 + place * len(UNITS[s][k]) + i] = (
+                        acc[h, starts[k] + shift * len(UNITS[s][k]) + i] = (
                             warped[ia, rows, lanes] * wa + warped[ib, rows, lanes] * wb
                         )
 

time: 62.7 us -> 62.5 us (level)
  no operation moved by 1% of the time
where the time goes in v5:
time: 62.5 us; the launch traced here: 62.3 us
  Pallas kernels  61.7 us (99%)
  between operations  0.64 us (1%)
    pallas_call x1, Pallas kernels, fused(): pl.pallas_call(kernel, out_shape=(jax.ShapeDtypeStruct((64, S), F32), jax...  60.1 us
    pallas_call x1, Pallas kernels, shards(): pl.pallas_call(store, out_shape=(jax.ShapeDtypeStruct((1, 64, S), F32), j...  1.59 us

profile of v5, /device:TPU:1, one launch (start us, length us, event | category | flops | bytes accessed | tf_op | source)
XLA Modules:
  0.0 62.3 jit_solution(10942600065871818773)
XLA Ops:
  0.6 60.1 %coadd.1 = (f32[64,512]{1,0:T(8,128)}, f32[4,128]{1,0:T(4,128)}, f32[8,512]{1,0:T(8,128)}) custom-call(s32[8]{0:T(128)} %patch_sm.1, bf16[1,8]{1,0:T(2,128)(2,1)} %bitcast.5, bf16[8,512,512]{2,1,0:T(8,128)(2,1)} %img_hbm.1, bf16[8,512,512]{2,1,0:T(8,128)(2,1)} %wr_hbm.1, bf16[8,512,512]{2,1,0:T(8,128)(2,1)} %wc_hbm.1, f32[512,512]{1,0:T(8,128)} %bitcast.3, ...), custom_call_target="tpu_custom_call" | custom-call | tf_op jit(solution)/shard_map/coadd/pallas_call | solution.py:484
  60.7 1.6 %store.1 = (f32[1,64,512]{2,1,0:T(8,128)}, f32[4]{0:T(128)}, f32[8,512]{1,0:T(8,128)}) custom-call(f32[64,512]{1,0:T(8,128)} %get-tuple-element.6.coadd_in, f32[4,128]{1,0:T(4,128)} %get-tuple-element.7.zp_in, f32[8,512]{1,0:T(8,128)} %get-tuple-element.8.resid_in), custom_call_target="tpu_custom_call" | custom-call | tf_op jit(solution)/shard_map/store/pallas_call | solution.py:551

commit v6 on v5

--- a/solution.py
+++ b/solution.py
@@ -14,7 +14,7 @@
 MESH = pl.DeviceIdType.MESH
 
 ORDER = ("x0", "y0", "z0", "x1", "y1", "z1")
-UNITS = (((0, 1), (2, 3), (4, 5), (6, 7), (8,), (9,)), ((10,), (11,), (12,), (13,), (14,), (15,)))
+UNITS = (((0, 1), (2, 3), (4,), (5,), (6,), (7,)), ((8,), (9,), (10, 11), (12, 13), (14,), (15,)))
 
 
 def gray(c):
@@ -82,6 +82,26 @@
     @pl.loop(1, NV)
     def _(o):
         pl.semaphore_signal(barrier, inc=1, device_id={"visit": (v + o) % NV, "patch": me}, device_id_type=MESH)
+
+    bases = {}
+    for k in range(6):
+        bases[k, 0] = 0
+        for j in range(6):
+            bases[k, j + 1] = bases[k, j] + side[ORDER[(k + j) % 6]] * (32 >> j)
+    lasts = {}
+    for k in range(6):
+        for e in range(1, 8):
+            place = bases[k, 3]
+            where = {"x": x, "y": y, "z": z}
+            for i in range(3):
+                d = ORDER[(k + 3 + i) % 6]
+                bit = side[d]
+                if e >> (2 - i) & 1:
+                    bit = 1 - bit
+                    c = where[d[0]]
+                    where[d[0]] = flip0(c) if d[1] == "0" else 3 - c
+                place = place + bit * (4 >> i)
+            lasts[k, e] = (place, (where["x"] * 2 + core, where["y"] * 4 + where["z"]))
 
     flips = {"x": (flip0(x), 3 - x), "y": (flip0(y), 3 - y), "z": (flip0(z), 3 - z)}
     met = set()
@@ -238,6 +258,8 @@
     bufs = (r0, r1, r2)
 
     def base_of(k, j):
+        if (k, j) in bases:
+            return bases[k, j]
         base = 0
         for i in range(j):
             base = base + side[ORDER[(k + i) % 6]] * (32 >> i)
@@ -261,17 +283,7 @@
             acc[core, at_] = acc[core, at_] + bufs[j][part(s, k, half, i * step, step)]
 
     def last_copy(s, k, e):
-        place = base_of(k, 3)
-        where = {"x": x, "y": y, "z": z}
-        for i in range(3):
-            d = ORDER[(k + 3 + i) % 6]
-            bit = side[d]
-            if e >> (2 - i) & 1:
-                bit = 1 - bit
-                c = where[d[0]]
-                where[d[0]] = flip0(c) if d[1] == "0" else 3 - c
-            place = place + bit * (4 >> i)
-        there = (where["x"] * 2 + core, where["y"] * 4 + where["z"])
+        place, there = lasts[k, e]
         return remote(
             acc.at[core, part(s, k, 64, place, 1)], fin.at[part(s, k, 8, e, 1)],
             fsem_s.at[s * 6 + k, e], fsem_r.at[s * 6 + k, e], there,

time: 62.5 us -> 62.7 us (level)
  no operation moved by 1% of the time
where the time goes in v6:
time: 62.7 us; the launch traced here: 62.5 us
  Pallas kernels  61.9 us (99%)
  between operations  0.64 us (1%)
    pallas_call x1, Pallas kernels, fused(): pl.pallas_call(kernel, out_shape=(jax.ShapeDtypeStruct((64, S), F32), jax...  60.3 us
    pallas_call x1, Pallas kernels, shards(): pl.pallas_call(store, out_shape=(jax.ShapeDtypeStruct((1, 64, S), F32), j...  1.59 us

profile of v6, /device:TPU:1, one launch (start us, length us, event | category | flops | bytes accessed | tf_op | source)
XLA Modules:
  0.0 62.5 jit_solution(3495990140472114814)
XLA Ops:
  0.6 60.3 %coadd.1 = (f32[64,512]{1,0:T(8,128)}, f32[4,128]{1,0:T(4,128)}, f32[8,512]{1,0:T(8,128)}) custom-call(s32[8]{0:T(128)} %patch_sm.1, bf16[1,8]{1,0:T(2,128)(2,1)} %bitcast.5, bf16[8,512,512]{2,1,0:T(8,128)(2,1)} %img_hbm.1, bf16[8,512,512]{2,1,0:T(8,128)(2,1)} %wr_hbm.1, bf16[8,512,512]{2,1,0:T(8,128)(2,1)} %wc_hbm.1, f32[512,512]{1,0:T(8,128)} %bitcast.3, ...), custom_call_target="tpu_custom_call" | custom-call | tf_op jit(solution)/shard_map/coadd/pallas_call | solution.py:496
  60.9 1.6 %store.1 = (f32[1,64,512]{2,1,0:T(8,128)}, f32[4]{0:T(128)}, f32[8,512]{1,0:T(8,128)}) custom-call(f32[64,512]{1,0:T(8,128)} %get-tuple-element.6.coadd_in, f32[4,128]{1,0:T(4,128)} %get-tuple-element.7.zp_in, f32[8,512]{1,0:T(8,128)} %get-tuple-element.8.resid_in), custom_call_target="tpu_custom_call" | custom-call | tf_op jit(solution)/shard_map/store/pallas_call | solution.py:563
